TPU v7x, 32 devices: a whole 2x2x4 slice. The times are simulated.
32 devices in a mesh: groups: 2 (over y), rows: 4 (over z), cols: 4 (over x, core).
Axes of the slice: x: 2, y: 2, z: 4, core: 2. Of those that a mesh axis runs over, the one named last changes fastest.
Arguments:
- queries: bfloat16 [4096, 1024], P(('groups', 'rows', 'cols')), parts along dimension 0, may hold values from -4.25 to 4.25
- keys: bfloat16 [4096, 128], P(('groups', 'rows', 'cols')), parts along dimension 0, may hold values from -4.25 to 4.25
- values: bfloat16 [4096, 128], P(('groups', 'rows', 'cols')), parts along dimension 0, may hold values from -6 to 6
- positions: int32 [4096], P(('groups', 'rows', 'cols')), parts along dimension 0, may hold values from 0 to 2047, as said below
Outputs:
- attended: bfloat16 [4096, 1024], P(('groups', 'rows', 'cols')), parts along dimension 0
There are 2 independent parts, one for each index of `groups`. A program takes and returns all parts, laid end to end along the dimension named above; each array names one. Nothing has to cross between parts.
Inputs may be any that keep to these rules, and one draw needn't show every extreme that they name: `positions`: a permutation of 0 to 2047.
All inputs are finite; a program needn't handle non-finite values.
Results may differ from a plain program's by a relative error of at most 0.015.
Values may be sent and summed in bfloat16 or wider, within the bound.
No kernel may reach another device: no remote copies, remote signals or barrier semaphores. Data moves between devices by JAX's collectives and lax.ppermute only.
A program may use at most 64 MiB of HBM per device.

v0:
```python
import math

import jax
import jax.numpy as jnp
from jax import lax
from jax.sharding import PartitionSpec as P

HEADS = 8
HEAD_DIM = 128


neg_fill = -1e30
tile_cap = 512


def make_absorb(query_heads, query_pos):
    scale = query_heads.shape[2] ** (-0.5)

    def absorb_tile(state, tile):
        key_tile, value_tile, pos_tile = tile
        run_max, run_sum, totals = state
        scores = (
            jnp.einsum("qhd,kd->qhk", query_heads, key_tile, preferred_element_type=jnp.float32)
            * scale
        )
        visible = pos_tile[None, None, :] <= query_pos[:, None, None]
        tile_max = jnp.max(jnp.where(visible, scores, neg_fill), axis=2)
        new_max = jnp.maximum(run_max, tile_max)
        weights = jnp.where(visible, jnp.exp(scores - new_max[:, :, None]), 0.0).astype(
            jnp.bfloat16
        )
        factor = jnp.exp(run_max - new_max)
        run_sum = run_sum * factor + jnp.sum(weights.astype(jnp.float32), axis=2)
        totals = totals * factor[:, :, None] + jnp.einsum(
            "qhk,kd->qhd", weights, value_tile, preferred_element_type=jnp.float32
        )
        return ((new_max, run_sum, totals), None)

    def absorb(carry, piece, start):
        key_part, value_part, key_pos = piece
        length = key_part.shape[0]
        tile_rows = math.gcd(length, tile_cap)
        tiles = length // tile_rows
        tiled = (
            key_part.reshape(tiles, tile_rows, key_part.shape[1]),
            value_part.reshape(tiles, tile_rows, value_part.shape[1]),
            key_pos.reshape(tiles, tile_rows),
        )
        carry, unused = lax.scan(absorb_tile, carry, tiled)
        return carry

    return absorb


def start_state(query_rows):
    return (
        jnp.full((query_rows, HEADS), neg_fill, jnp.float32),
        jnp.zeros((query_rows, HEADS), jnp.float32),
        jnp.zeros((query_rows, HEADS, HEAD_DIM), jnp.float32),
    )


def shards(queries, keys, values, positions):
    own_rows = queries.shape[0]
    query_heads = queries.reshape(own_rows, HEADS, HEAD_DIM)
    absorb = make_absorb(query_heads, positions)
    partial_value = absorb(
        start_state(own_rows),
        (
            lax.all_gather(keys, ("rows", "cols"), axis=0, tiled=True),
            lax.all_gather(values, ("rows", "cols"), axis=0, tiled=True),
            lax.all_gather(positions, ("rows", "cols"), axis=0, tiled=True),
        ),
        jnp.int32(0),
    )
    denominators = partial_value[1]
    numerators = partial_value[2]
    result = numerators / denominators[:, :, None]
    return result.astype(jnp.bfloat16).reshape(own_rows, HEADS * HEAD_DIM)


def solution(mesh):
    return jax.shard_map(
        shards,
        mesh=mesh,
        in_specs=(
            P(("groups", "rows", "cols"), None),
            P(("groups", "rows", "cols"), None),
            P(("groups", "rows", "cols"), None),
            P(("groups", "rows", "cols")),
        ),
        out_specs=P(("groups", "rows", "cols"), None),
        check_vma=False,
    )
```

profile of v0, /device:TPU:0, one launch (start us, length us, event | category | flops | bytes accessed | tf_op | source)
XLA Modules:
  0.0 79.0 jit_solution(12924049087476790847)
XLA Ops:
  0.0 0.0 copy-start
  0.0 24.9 %all_gather.10 = bf16[2048,128]{1,0:T(8,128)(2,1)S(1)} all-gather(bf16[128,128]{1,0:T(8,128)(2,1)} %param.7), channel_id=1, replica_groups=mesh['groups'=2,'rows'=4,'cols'=4] {'rows','cols'}, dimensions={0}, use_global_device_ids=true | all-gather | bytes 557056 | tf_op jit(solution)/shard_map/all_gather | solution.py:70
  24.9 20.5 %all_gather.11 = bf16[2048,128]{1,0:T(8,128)(2,1)} all-gather(bf16[128,128]{1,0:T(8,128)(2,1)} %param.8), channel_id=1, replica_groups=mesh['groups'=2,'rows'=4,'cols'=4] {'rows','cols'}, dimensions={0}, use_global_device_ids=true | all-gather | bytes 557056 | tf_op jit(solution)/shard_map/all_gather | solution.py:71
  45.4 1.1 %copy.12 = bf16[128,1024]{0,1:T(8,128)(2,1)S(1)} copy(bf16[128,1024]{1,0:T(8,128)(2,1)} %param.6) | data formatting | bytes 524288 | tf_op args[0]
  46.6 0.2 copy.13
  46.8 0.0 copy-done
  46.8 19.0 %all-gather = s32[16,1,128]{2,1,0:T(1,128)S(1)} all-gather(s32[1,1,128]{2,1,0:T(1,128)S(1)} %bitcast.53), channel_id=1, replica_groups=mesh['groups'=2,'rows'=4,'cols'=4] {'rows','cols'}, dimensions={0}, use_global_device_ids=true | all-gather | bytes 8704 | tf_op jit(solution)/shard_map/all_gather | solution.py:72
  65.7 0.5 broadcast.55
  66.2 0.7 reduce.3
  66.9 11.2 %while.15 = (s32[]{:T(128)}, f32[128,8]{0,1:T(8,128)S(1)}, f32[128,8]{0,1:T(8,128)S(1)}, f32[128,8,128]{2,0,1:T(8,128)S(1)}, s32[4,512]{1,0:T(4,128)S(1)}, /*ind...) while((s32[]{:T(128)}, f32[128,8]{0,1:T(8,128)S(1)}, ...), condition=%wide.region_3.4_spmd.clone, body=%wide.region_0.3_spmd.clone.sunk | while | flops 275715072 | bytes 8199297 | solution.py:49
  67.0 0.1 broadcast_compare_fusion.2
  67.1 0.5 fusion.24
  67.6 0.4 convert_reduce_fusion.2
  68.1 1.7 %convolution_add_fusion.2 = f32[128,8,128]{2,0,1:T(8,128)S(1)} fusion(f32[128,8,128]{2,0,1:T(8,128)S(1)} %get-tuple-element.202, f32[128,8]{0,1:T(8,128)S(1)} %get-tuple-element.187, pred[]{:T(512)S(6)} %compare.3, bf16[4,512,128]{2,1,0:T(8,128)(2,1)} %get-tuple-element.218, s32[]{:T(128)} %get-tuple-element.199, ...), kind=kOutput, calls=%fused_computation.7.clone.1 | convolution fusion | flops 136708096 | bytes 3351041 | tf_op jit(solution)/shard_map/while/body/eval_jaxpr/qhk,kd->qhd/dot_general | solution.py:34
  69.8 0.1 broadcast_compare_fusion.2
  69.9 0.5 fusion.24
  70.4 0.4 convert_reduce_fusion.2
  70.8 1.7 %convolution_add_fusion.2 = f32[128,8,128]{2,0,1:T(8,128)S(1)} fusion(f32[128,8,128]{2,0,1:T(8,128)S(1)} %get-tuple-element.202, f32[128,8]{0,1:T(8,128)S(1)} %get-tuple-element.187, pred[]{:T(512)S(6)} %compare.3, bf16[4,512,128]{2,1,0:T(8,128)(2,1)} %get-tuple-element.218, s32[]{:T(128)} %get-tuple-element.199, ...), kind=kOutput, calls=%fused_computation.7.clone.1 | convolution fusion | flops 136708096 | bytes 3351041 | tf_op jit(solution)/shard_map/while/body/eval_jaxpr/qhk,kd->qhd/dot_general | solution.py:34
  72.6 0.1 broadcast_compare_fusion.2
  72.7 0.5 fusion.24
  73.2 0.4 convert_reduce_fusion.2
  73.6 1.7 %convolution_add_fusion.2 = f32[128,8,128]{2,0,1:T(8,128)S(1)} fusion(f32[128,8,128]{2,0,1:T(8,128)S(1)} %get-tuple-element.202, f32[128,8]{0,1:T(8,128)S(1)} %get-tuple-element.187, pred[]{:T(512)S(6)} %compare.3, bf16[4,512,128]{2,1,0:T(8,128)(2,1)} %get-tuple-element.218, s32[]{:T(128)} %get-tuple-element.199, ...), kind=kOutput, calls=%fused_computation.7.clone.1 | convolution fusion | flops 136708096 | bytes 3351041 | tf_op jit(solution)/shard_map/while/body/eval_jaxpr/qhk,kd->qhd/dot_general | solution.py:34
  75.4 0.1 broadcast_compare_fusion.2
  75.5 0.5 fusion.24
  76.0 0.4 convert_reduce_fusion.2
  76.4 1.7 %convolution_add_fusion.2 = f32[128,8,128]{2,0,1:T(8,128)S(1)} fusion(f32[128,8,128]{2,0,1:T(8,128)S(1)} %get-tuple-element.202, f32[128,8]{0,1:T(8,128)S(1)} %get-tuple-element.187, pred[]{:T(512)S(6)} %compare.3, bf16[4,512,128]{2,1,0:T(8,128)(2,1)} %get-tuple-element.218, s32[]{:T(128)} %get-tuple-element.199, ...), kind=kOutput, calls=%fused_computation.7.clone.1 | convolution fusion | flops 136708096 | bytes 3351041 | tf_op jit(solution)/shard_map/while/body/eval_jaxpr/qhk,kd->qhd/dot_general | solution.py:34
  78.1 0.9 %copy_bitcast_fusion = bf16[128,1024]{1,0:T(8,128)(2,1)} fusion(f32[128,8,128]{2,0,1:T(8,128)S(1)} %get-tuple-element.53, f32[128,8]{0,1:T(8,128)S(1)} %get-tuple-element.54), kind=kLoop, calls=%fused_computation.23 | loop fusion | flops 262144 | bytes 790528 | tf_op jit(solution)/shard_map/reshape | solution.py:79
  (20 shorter events, 0.1 us)
Async XLA Ops:
  0.0 46.8 %copy-start = (s32[128]{0:T(128)S(1)}, s32[128]{0:T(128)}, u32[]{:S(2)}) copy-start(s32[128]{0:T(128)} %param.9) | copy-start | bytes 1540
where the time goes:
time: 79.3 us; the launch traced here: 79 us
  blocking collectives  64.4 us (81%)
  matrix products  8.48 us (11%)
  other arithmetic  3.95 us (5%)
  local copies, waits for them, and re-layouts  1.86 us (2%)
    all_gather x1, blocking collectives, shards(): lax.all_gather(keys, ('rows', 'cols'), axis=0, tiled=True)  24.9 us
    all_gather x1, blocking collectives, shards(): lax.all_gather(values, ('rows', 'cols'), axis=0, tiled=True)  20.5 us
    all_gather x1, blocking collectives, shards(): lax.all_gather(positions, ('rows', 'cols'), axis=0, tiled=True)  19 us
    dot_general x4, matrix products, absorb_tile(): jnp.einsum('qhk,kd->qhd', weights, value_tile, preferred_element_type=jnp...  6.65 us
    dot_general x4, matrix products, absorb_tile(): jnp.einsum('qhd,kd->qhk', query_heads, key_tile, preferred_element_type=j...  1.82 us
    reduce_sum x4, other arithmetic, absorb_tile(): run_sum = run_sum * factor + jnp.sum(weights.astype(jnp.float32), axis=2)  1.76 us

commit v1 on v0

v1 whole, which is shorter than its diff:
```python
import functools
import math

import jax
import jax.numpy as jnp
from jax import lax
from jax.experimental import pallas as pl
from jax.experimental.pallas import tpu as pltpu
from jax.sharding import PartitionSpec as P

HEADS = 8
HEAD_DIM = 128
LANES = 128
POS_ROWS = 16
HIGH_SHIFT = 7
LOW_MASK = 127

den_low = 1e-18
den_high = 1e37
neg_fill = -1e30
vmem_bytes = 16 * 1024 * 1024


VMEM = pl.BlockSpec(memory_space=pltpu.VMEM)


def call(kernel, out_shape, operands, scratch=(), flops=0):
    size = sum(x.size * x.dtype.itemsize for x in operands)
    return pl.pallas_call(
        kernel,
        out_shape=out_shape,
        in_specs=[VMEM] * len(operands),
        out_specs=jax.tree.map(lambda s: VMEM, out_shape),
        scratch_shapes=scratch,
        compiler_params=pltpu.CompilerParams(vmem_limit_bytes=vmem_bytes),
        cost_estimate=pl.CostEstimate(flops=flops, bytes_accessed=size, transcendentals=0),
    )(*operands)


def pack_kernel(key_ref, value_ref, pos_ref, q_ref, block_ref, qs_ref):
    tokens = key_ref.shape[0]
    block_ref[0, :tokens, :] = key_ref[...]
    block_ref[0, tokens : 2 * tokens, :] = value_ref[...]
    row = lax.broadcasted_iota(jnp.int32, (POS_ROWS, LANES), 0)
    tile = jnp.zeros((POS_ROWS, LANES), jnp.float32)
    for j in range(tokens // LANES):
        pos = pos_ref[:, j * LANES : (j + 1) * LANES]
        high = (pos >> HIGH_SHIFT).astype(jnp.float32)
        low = (pos & LOW_MASK).astype(jnp.float32)
        tile = jnp.where(row == 2 * j, jnp.broadcast_to(high, tile.shape), tile)
        tile = jnp.where(row == 2 * j + 1, jnp.broadcast_to(low, tile.shape), tile)
    block_ref[0, 2 * tokens :, :] = tile.astype(block_ref.dtype)
    for h in range(HEADS):
        qs_ref[h * tokens : (h + 1) * tokens, :] = q_ref[:, h * HEAD_DIM : (h + 1) * HEAD_DIM]


def block_rows(ref):
    return (ref.shape[1] - POS_ROWS) // 2


def keys_of(ref, i):
    return ref[i, : block_rows(ref), :]


def values_of(ref, i):
    rows = block_rows(ref)
    return jnp.concatenate(
        [ref[i, rows : 2 * rows, :], jnp.ones((rows, HEAD_DIM), jnp.bfloat16)], axis=1
    )


def visible_of(ref, i, query_pos):
    rows = block_rows(ref)
    parts = ref[i, 2 * rows :, :].astype(jnp.float32)
    return jnp.concatenate(
        [
            parts[2 * j : 2 * j + 1] * (LOW_MASK + 1) + parts[2 * j + 1 : 2 * j + 2] <= query_pos
            for j in range(rows // LANES)
        ],
        axis=1,
    )


def dot_keys(q, keys):
    return lax.dot_general(
        q, keys, (((1,), (1,)), ((), ())), preferred_element_type=jnp.float32
    )


def absorb(qs_ref, query_pos, total, blocks, at, stack):
    pre = HEAD_DIM ** (-0.5) * math.log2(math.e)
    q = qs_ref[at, :]
    for j in range(0, len(blocks), 2):
        group = blocks[j : j + 2]
        scores = dot_keys(q, jnp.concatenate([keys_of(*b) for b in group], axis=0))
        mask = jnp.concatenate([visible_of(*b, query_pos) for b in group], axis=1)
        mask = jnp.concatenate([mask] * stack, axis=0)
        weights = jnp.where(mask, jnp.exp2(scores * pre), 0.0).astype(jnp.bfloat16)
        part = jnp.dot(
            weights,
            jnp.concatenate([values_of(*b) for b in group], axis=0),
            preferred_element_type=jnp.float32,
        )
        total = part if total is None else total + part
    return total


def accumulate(qs_ref, query_pos, before, after, pieces):
    stack = 4 if HEADS % 4 == 0 else 1
    tokens = query_pos.shape[0]
    span = stack * tokens
    small = sum(p.shape[0] for p in pieces) <= 8
    for r in range(HEADS // stack):
        at = slice(r * span, (r + 1) * span)
        start = None if before is None else before[at, :]
        if small:
            blocks = [(p, i) for p in pieces for i in range(p.shape[0])]
            after[at, :] = absorb(qs_ref, query_pos, start, blocks, at, stack)
            continue
        after[at, :] = jnp.zeros((span, 2 * HEAD_DIM), jnp.float32) if start is None else start
        for p in pieces:

            def pair(i, carry, p=p):
                blocks = [(p, 2 * i), (p, 2 * i + 1)]
                after[at, :] = absorb(qs_ref, query_pos, after[at, :], blocks, at, stack)
                return carry

            lax.fori_loop(0, p.shape[0] // 2, pair, 0)


def bundle(pieces, out_ref):
    at = 0
    for p in pieces:
        out_ref[at : at + p.shape[0]] = p[...]
        at += p.shape[0]


def first_kernel(count, qs_ref, pos_ref, *refs):
    pieces = refs[:count]
    acc_ref, bundle_ref, qpos_ref = refs[count:]
    tokens = pos_ref.shape[1]
    bundle(pieces, bundle_ref)
    qpos_ref[...] = jnp.transpose(
        jnp.broadcast_to(pos_ref[...].astype(jnp.float32), (LANES, tokens))
    )
    accumulate(qs_ref, qpos_ref[...], None, acc_ref, pieces)


def next_kernel(count, qs_ref, qpos_ref, before_ref, *refs):
    pieces = refs[:count]
    if len(refs) > count + 1:
        bundle(pieces, refs[count + 1])
    accumulate(qs_ref, qpos_ref[...], before_ref, refs[count], pieces)


def last_kernel(count, qs_ref, qpos_ref, before_ref, *refs):
    pieces = refs[:count]
    o_ref, acc_ref = refs[count:]
    query_pos = qpos_ref[...]
    tokens = query_pos.shape[0]
    scale = HEAD_DIM ** (-0.5)
    accumulate(qs_ref, query_pos, before_ref, acc_ref, pieces[:1])

    def store():
        for h in range(HEADS):
            part = acc_ref[h * tokens : (h + 1) * tokens, :]
            o_ref[:, h * HEAD_DIM : (h + 1) * HEAD_DIM] = (
                part[:, :HEAD_DIM] / part[:, HEAD_DIM:]
            ).astype(o_ref.dtype)

    store()
    den = acc_ref[:, HEAD_DIM:]
    good = (den >= den_low) & (den <= den_high)

    @pl.when(jnp.min(jnp.where(good, 1.0, 0.0)) < 0.5)
    def _():
        def one_head(h, carry):
            at = pl.ds(pl.multiple_of(h * tokens, tokens), tokens)
            q = qs_ref[at, :]
            top = jnp.full((tokens, 1), neg_fill, jnp.float32)
            for ref in pieces:

                def raise_top(i, top, ref=ref):
                    s = dot_keys(q, keys_of(ref, i)) * scale
                    s = jnp.where(visible_of(ref, i, query_pos), s, neg_fill)
                    return jnp.maximum(top, jnp.max(s, axis=1, keepdims=True))

                top = lax.fori_loop(0, ref.shape[0], raise_top, top)
            total = jnp.zeros((tokens, 2 * HEAD_DIM), jnp.float32)
            for ref in pieces:

                def add(i, total, ref=ref):
                    s = dot_keys(q, keys_of(ref, i)) * scale
                    w = jnp.where(visible_of(ref, i, query_pos), jnp.exp(s - top), 0.0)
                    return total + jnp.dot(
                        w.astype(jnp.bfloat16),
                        values_of(ref, i),
                        preferred_element_type=jnp.float32,
                    )

                total = lax.fori_loop(0, ref.shape[0], add, total)
            acc_ref[at, :] = total
            return carry

        lax.fori_loop(0, HEADS, one_head, 0)
        store()


def swap(x, axis, size, bit):
    return lax.ppermute(x, axis, [(i, i ^ bit) for i in range(size)])


def attention(rows, cols, queries, keys, values, positions):
    tokens = queries.shape[0]
    pos = positions.reshape(1, tokens)
    block = jax.ShapeDtypeStruct((1, 2 * tokens + POS_ROWS, HEAD_DIM), jnp.bfloat16)
    in_hbm = functools.partial(pltpu.with_memory_space_constraint, memory_space=pltpu.HBM)
    own, qs = call(
        pack_kernel,
        (block, jax.ShapeDtypeStruct((HEADS * tokens, HEAD_DIM), jnp.bfloat16)),
        [in_hbm(x) for x in (keys, values, pos, queries)],
    )
    acc = jax.ShapeDtypeStruct((HEADS * tokens, 2 * HEAD_DIM), jnp.float32)
    qpos = jax.ShapeDtypeStruct((tokens, LANES), jnp.float32)

    def bundled(pieces):
        return jax.ShapeDtypeStruct(
            (sum(p.shape[0] for p in pieces),) + pieces[0].shape[1:], jnp.bfloat16
        )

    def work(pieces):
        return 4 * HEADS * tokens * HEAD_DIM * tokens * sum(p.shape[0] for p in pieces)

    def further(before, pieces, with_bundle):
        out = (acc, bundled(pieces)) if with_bundle else (acc,)
        return call(
            functools.partial(next_kernel, len(pieces)), out,
            [qs, query_pos, before, *pieces], flops=work(pieces),
        )

    bit = rows // 2
    while bit >= 4:
        own = jnp.concatenate([own, swap(own, "rows", rows, bit)], axis=0)
        bit //= 2
    z2 = swap(own, "rows", rows, 2)
    z1 = swap(own, "rows", rows, 1)
    xo = swap(own, "cols", cols, 2)
    z3 = swap(z2, "rows", rows, 1)
    xz2 = swap(z2, "cols", cols, 2)
    xz1 = swap(z1, "cols", cols, 2)
    near = [own, z2, z1, xo]
    acc1, b1, query_pos = call(
        functools.partial(first_kernel, len(near)),
        (acc, bundled(near), qpos),
        [qs, pos, *near], flops=work(near),
    )
    xz3 = swap(z3, "cols", cols, 2)
    cb1 = swap(b1, "cols", cols, 1)
    acc2, b2 = further(acc1, [z3, xz2, xz1], True)
    cb2 = swap(b2, "cols", cols, 1)
    (acc3,) = further(acc2, [cb1], False)
    c3 = swap(xz3, "cols", cols, 1)
    (acc4,) = further(acc3, [cb2, xz3], False)
    pieces = [c3, b1, b2, xz3, cb1, cb2]
    return call(
        functools.partial(last_kernel, len(pieces)),
        jax.ShapeDtypeStruct(queries.shape, jnp.bfloat16),
        [qs, query_pos, acc4, *pieces],
        scratch=[pltpu.VMEM(acc.shape, acc.dtype)], flops=work([c3]),
    )


def solution(mesh):
    rows, cols = mesh.shape["rows"], mesh.shape["cols"]

    def shards(*arrays):
        return attention(rows, cols, *arrays)

    return jax.shard_map(
        shards,
        mesh=mesh,
        in_specs=(
            P(("groups", "rows", "cols"), None),
            P(("groups", "rows", "cols"), None),
            P(("groups", "rows", "cols"), None),
            P(("groups", "rows", "cols")),
        ),
        out_specs=P(("groups", "rows", "cols"), None),
        check_vma=False,
    )
```

time: 79.3 us -> 95.1 us (1.20)
  the two profiles are of different devices: /device:TPU:0 before, /device:TPU:1 now
where the time goes in v1:
time: 95.1 us; the launch traced here: 94.9 us
  Pallas kernels  73.8 us (78%)
  starting transfers between devices  13.1 us (14%)
  waiting for transfers between devices  8.02 us (8%)
    pallas_call x6, Pallas kernels, call(): pl.pallas_call(kernel, out_shape=out_shape, in_specs=[VMEM] * len(operand...  73.8 us
    ppermute x10, starting transfers between devices, swap(): return lax.ppermute(x, axis, [(i, i ^ bit) for i in range(size)])  13.1 us
    ppermute x10, waiting for transfers between devices, swap(): return lax.ppermute(x, axis, [(i, i ^ bit) for i in range(size)])  8.02 us
  transfers between devices with their start and end apart: 10, of which 5 were waited for; matrix products, arithmetic and copies ran while one was open for 0% of the time, Pallas kernels for 3%

profile of v1, /device:TPU:1, one launch (start us, length us, event | category | flops | bytes accessed | tf_op | source)
XLA Modules:
  0.0 94.9 jit_solution(8964493313900802578)
XLA Ops:
  0.0 1.1 %shard_map.46 = (bf16[1,272,128]{2,1,0:T(8,128)(2,1)S(1)}, bf16[1024,128]{1,0:T(8,128)(2,1)S(1)}) custom-call(bf16[128,128]{1,0:T(8,128)(2,1)} %key_ref.1, bf16[128,128]{1,0:T(8,128)(2,1)} %value_ref.1, s32[1,128]{1,0:T(1,128)} %bitcast.1, bf16[128,1024]{1,0:T(8,128)(2,1)} %q_ref.1), custom_call_target="tpu_custom_call" | custom-call | bytes 328192 | tf_op jit(solution)/shard_map/pallas_call | solution.py:29
  1.1 0.0 copy-start
  1.1 3.2 %collective-permute-start = (bf16[1,272,128]{2,1,0:T(8,128)(2,1)S(1)}, bf16[1,272,128]{2,1,0:T(8,128)(2,1)S(1)}, u32[]{:S(2)}, u32[]{:S(2)}) collective-permute-start(bf16[1,272,128]{2,1,0:T(8,128)(2,1)S(1)} %get-tuple-element.13.refs_0_), channel_id=1, source_target_pairs={{0,8},{4,12},{8,0},{12,4},{1,9},{5,13},{9,1},{13,5},{2,10},{6,14},... | collective-permute-start | bytes 208904 | tf_op jit(solution)/shard_map/ppermute | solution.py:210
  4.3 1.3 %collective-permute-start.1 = (bf16[1,272,128]{2,1,0:T(8,128)(2,1)S(1)}, bf16[1,272,128]{2,1,0:T(8,128)(2,1)S(1)}, u32[]{:S(2)}, u32[]{:S(2)}) collective-permute-start(bf16[1,272,128]{2,1,0:T(8,128)(2,1)S(1)} %get-tuple-element.13.refs_0_), channel_id=1, source_target_pairs={{0,4},{4,0},{8,12},{12,8},{1,5},{5,1},{9,13},{13,9},{2,6},{6,2},{1... | collective-permute-start | bytes 208904 | tf_op jit(solution)/shard_map/ppermute | solution.py:210
  5.6 1.2 %collective-permute-start.2 = (bf16[1,272,128]{2,1,0:T(8,128)(2,1)S(1)}, bf16[1,272,128]{2,1,0:T(8,128)(2,1)S(1)}, u32[]{:S(2)}, u32[]{:S(2)}) collective-permute-start(bf16[1,272,128]{2,1,0:T(8,128)(2,1)S(1)} %get-tuple-element.13.refs_0_), channel_id=1, source_target_pairs={{0,2},{1,3},{2,0},{3,1},{4,6},{5,7},{6,4},{7,5},{8,10},{9,11},{10,... | collective-permute-start | bytes 208904 | tf_op jit(solution)/shard_map/ppermute | solution.py:210
  6.8 0.0 collective-permute-done.refs_1_
  6.8 1.2 %collective-permute-done.1.refs_2_ = bf16[1,272,128]{2,1,0:T(8,128)(2,1)S(1)} collective-permute-done((bf16[1,272,128]{2,1,0:T(8,128)(2,1)S(1)}, bf16[1,272,128]{2,1,0:T(8,128)(2,1)S(1)}, u32[]{:S(2)}, u32[]{:S(2)}) %collective-permute-start.1) | collective-permute-done | bytes 69664 | tf_op jit(solution)/shard_map/ppermute | solution.py:210
  8.0 1.0 %collective-permute-done.2.refs_3_ = bf16[1,272,128]{2,1,0:T(8,128)(2,1)S(1)} collective-permute-done((bf16[1,272,128]{2,1,0:T(8,128)(2,1)S(1)}, bf16[1,272,128]{2,1,0:T(8,128)(2,1)S(1)}, u32[]{:S(2)}, u32[]{:S(2)}) %collective-permute-start.2) | collective-permute-done | bytes 69664 | tf_op jit(solution)/shard_map/ppermute | solution.py:210
  9.0 0.0 copy-done
  9.0 1.0 %shard_map.47 = (f32[1024,256]{1,0:T(8,128)S(1)}, bf16[4,272,128]{2,1,0:T(8,128)(2,1)S(1)}, f32[128,128]{1,0:T(8,128)S(1)}) custom-call(bf16[1024,128]{1,0:T(8,128)(2,1)S(1)} %get-tuple-element.12.qs_ref, s32[1,128]{1,0:T(1,128)S(1)} %bitcast.2, bf16[1,272,128]{2,1,0:T(8,128)(2,1)S(1)} %get-tuple-element.13.refs_0_, ...), custom_call_target="tpu_custom_call" | custom-call | flops 268435456 | bytes 541184 | tf_op jit(solution)/shard_map/pallas_call | solution.py:29
  10.0 2.2 %collective-permute-start.6 = (bf16[4,272,128]{2,1,0:T(8,128)(2,1)S(1)}, bf16[4,272,128]{2,1,0:T(8,128)(2,1)S(1)}, u32[]{:S(2)}, u32[]{:S(2)}) collective-permute-start(bf16[4,272,128]{2,1,0:T(8,128)(2,1)S(1)} %get-tuple-element.17.refs_1_), channel_id=1, source_target_pairs={{0,1},{1,0},{2,3},{3,2},{4,5},{5,4},{6,7},{7,6},{8,9},{9,8},{10,11... | collective-permute-start | bytes 835592 | tf_op jit(solution)/shard_map/ppermute | solution.py:210
  12.1 0.2 collective-permute-start.3
  12.3 1.2 %collective-permute-start.4 = (bf16[1,272,128]{2,1,0:T(8,128)(2,1)S(1)}, bf16[1,272,128]{2,1,0:T(8,128)(2,1)S(1)}, u32[]{:S(2)}, u32[]{:S(2)}) collective-permute-start(bf16[1,272,128]{2,1,0:T(8,128)(2,1)S(1)} %collective-permute-done.refs_1_), channel_id=1, source_target_pairs={{0,2},{1,3},{2,0},{3,1},{4,6},{5,7},{6,4},{7,5},{8,10},{9,11},{10,... | collective-permute-start | bytes 208904 | tf_op jit(solution)/shard_map/ppermute | solution.py:210
  13.5 0.3 collective-permute-start.5
  13.8 2.0 %collective-permute-done.3.refs_0_ = bf16[1,272,128]{2,1,0:T(8,128)(2,1)S(1)} collective-permute-done((bf16[1,272,128]{2,1,0:T(8,128)(2,1)S(1)}, bf16[1,272,128]{2,1,0:T(8,128)(2,1)S(1)}, u32[]{:S(2)}, u32[]{:S(2)}) %collective-permute-start.3) | collective-permute-done | bytes 69664 | tf_op jit(solution)/shard_map/ppermute | solution.py:210
  15.8 0.0 collective-permute-done.4.refs_1_
  15.8 1.2 %collective-permute-done.5.refs_2_ = bf16[1,272,128]{2,1,0:T(8,128)(2,1)S(1)} collective-permute-done((bf16[1,272,128]{2,1,0:T(8,128)(2,1)S(1)}, bf16[1,272,128]{2,1,0:T(8,128)(2,1)S(1)}, u32[]{:S(2)}, u32[]{:S(2)}) %collective-permute-start.5) | collective-permute-done | bytes 69664 | tf_op jit(solution)/shard_map/ppermute | solution.py:210
  17.0 0.9 shard_map.48
  18.0 1.5 %collective-permute-start.7 = (bf16[3,272,128]{2,1,0:T(8,128)(2,1)S(1)}, bf16[3,272,128]{2,1,0:T(8,128)(2,1)S(1)}, u32[]{:S(2)}, u32[]{:S(2)}) collective-permute-start(bf16[3,272,128]{2,1,0:T(8,128)(2,1)S(1)} %get-tuple-element.18.refs_2_), channel_id=1, source_target_pairs={{0,1},{1,0},{2,3},{3,2},{4,5},{5,4},{6,7},{7,6},{8,9},{9,8},{10,11... | collective-permute-start | bytes 626696 | tf_op jit(solution)/shard_map/ppermute | solution.py:210
  19.5 1.1 %collective-permute-start.8 = (bf16[1,272,128]{2,1,0:T(8,128)(2,1)S(1)}, bf16[1,272,128]{2,1,0:T(8,128)(2,1)S(1)}, u32[]{:S(2)}, u32[]{:S(2)}) collective-permute-start(bf16[1,272,128]{2,1,0:T(8,128)(2,1)S(1)} %collective-permute-done.3.refs_0_), channel_id=1, source_target_pairs={{0,2},{1,3},{2,0},{3,1},{4,6},{5,7},{6,4},{7,5},{8,10},{9,11},{10,... | collective-permute-start | bytes 208904 | tf_op jit(solution)/shard_map/ppermute | solution.py:210
  20.6 2.5 %collective-permute-done.8.refs_1_.refs_3_ = bf16[1,272,128]{2,1,0:T(8,128)(2,1)S(1)} collective-permute-done((bf16[1,272,128]{2,1,0:T(8,128)(2,1)S(1)}, bf16[1,272,128]{2,1,0:T(8,128)(2,1)S(1)}, u32[]{:S(2)}, u32[]{:S(2)}) %collective-permute-start.8) | collective-permute-done | bytes 69664 | tf_op jit(solution)/shard_map/ppermute | solution.py:210
  23.1 0.9 collective-permute-start.9
  24.1 0.0 collective-permute-done.6.refs_0_.refs_4_
  24.1 0.8 shard_map.49.before_ref
  24.9 0.0 collective-permute-done.7.refs_0_.refs_5_
  24.9 0.8 shard_map.50.before_ref
  25.7 0.0 collective-permute-done.9.refs_0_
  25.8 69.2 %shard_map.51 = bf16[128,1024]{1,0:T(8,128)(2,1)} custom-call(bf16[1024,128]{1,0:T(8,128)(2,1)S(1)} %get-tuple-element.12.qs_ref, f32[128,128]{1,0:T(8,128)S(1)} %get-tuple-element.14.qpos_ref, f32[1024,256]{1,0:T(8,128)S(1)} %shard_map.50.before_ref, bf16[1,272,128]{2,1,0:T(8,128)(2,1)S(1)} %collective-permute-done.9.refs_0_, ...), custom_call_target="tpu_custom_call" | custom-call | flops 67108864 | bytes 2490368 | tf_op jit(solution)/shard_map/pallas_call | solution.py:29
Async XLA Ops:
  1.1 8.0 %copy-start = (s32[128]{0:T(128)S(1)}, s32[128]{0:T(128)}, u32[]{:S(2)}) copy-start(s32[128]{0:T(128)} %param.7) | copy-start | bytes 1540
  1.1 5.7 %collective-permute-start = (bf16[1,272,128]{2,1,0:T(8,128)(2,1)S(1)}, bf16[1,272,128]{2,1,0:T(8,128)(2,1)S(1)}, u32[]{:S(2)}, u32[]{:S(2)}) collective-permute-start(bf16[1,272,128]{2,1,0:T(8,128)(2,1)S(1)} %get-tuple-element.13.refs_0_), channel_id=1, source_target_pairs={{0,8},{4,12},{8,0},{12,4},{1,9},{5,13},{9,1},{13,5},{2,10},{6,14},... | collective-permute-start | bytes 208904 | tf_op jit(solution)/shard_map/ppermute | solution.py:210
  4.3 3.7 %collective-permute-start.1 = (bf16[1,272,128]{2,1,0:T(8,128)(2,1)S(1)}, bf16[1,272,128]{2,1,0:T(8,128)(2,1)S(1)}, u32[]{:S(2)}, u32[]{:S(2)}) collective-permute-start(bf16[1,272,128]{2,1,0:T(8,128)(2,1)S(1)} %get-tuple-element.13.refs_0_), channel_id=1, source_target_pairs={{0,4},{4,0},{8,12},{12,8},{1,5},{5,1},{9,13},{13,9},{2,6},{6,2},{1... | collective-permute-start | bytes 208904 | tf_op jit(solution)/shard_map/ppermute | solution.py:210
  5.6 3.5 %collective-permute-start.2 = (bf16[1,272,128]{2,1,0:T(8,128)(2,1)S(1)}, bf16[1,272,128]{2,1,0:T(8,128)(2,1)S(1)}, u32[]{:S(2)}, u32[]{:S(2)}) collective-permute-start(bf16[1,272,128]{2,1,0:T(8,128)(2,1)S(1)} %get-tuple-element.13.refs_0_), channel_id=1, source_target_pairs={{0,2},{1,3},{2,0},{3,1},{4,6},{5,7},{6,4},{7,5},{8,10},{9,11},{10,... | collective-permute-start | bytes 208904 | tf_op jit(solution)/shard_map/ppermute | solution.py:210
  10.0 14.1 %collective-permute-start.6 = (bf16[4,272,128]{2,1,0:T(8,128)(2,1)S(1)}, bf16[4,272,128]{2,1,0:T(8,128)(2,1)S(1)}, u32[]{:S(2)}, u32[]{:S(2)}) collective-permute-start(bf16[4,272,128]{2,1,0:T(8,128)(2,1)S(1)} %get-tuple-element.17.refs_1_), channel_id=1, source_target_pairs={{0,1},{1,0},{2,3},{3,2},{4,5},{5,4},{6,7},{7,6},{8,9},{9,8},{10,11... | collective-permute-start | bytes 835592 | tf_op jit(solution)/shard_map/ppermute | solution.py:210
  12.1 3.7 %collective-permute-start.3 = (bf16[1,272,128]{2,1,0:T(8,128)(2,1)S(1)}, bf16[1,272,128]{2,1,0:T(8,128)(2,1)S(1)}, u32[]{:S(2)}, u32[]{:S(2)}) collective-permute-start(bf16[1,272,128]{2,1,0:T(8,128)(2,1)S(1)} %collective-permute-done.refs_1_), channel_id=1, source_target_pairs={{0,4},{4,0},{8,12},{12,8},{1,5},{5,1},{9,13},{13,9},{2,6},{6,2},{1... | collective-permute-start | bytes 208904 | tf_op jit(solution)/shard_map/ppermute | solution.py:210
  12.3 3.5 %collective-permute-start.4 = (bf16[1,272,128]{2,1,0:T(8,128)(2,1)S(1)}, bf16[1,272,128]{2,1,0:T(8,128)(2,1)S(1)}, u32[]{:S(2)}, u32[]{:S(2)}) collective-permute-start(bf16[1,272,128]{2,1,0:T(8,128)(2,1)S(1)} %collective-permute-done.refs_1_), channel_id=1, source_target_pairs={{0,2},{1,3},{2,0},{3,1},{4,6},{5,7},{6,4},{7,5},{8,10},{9,11},{10,... | collective-permute-start | bytes 208904 | tf_op jit(solution)/shard_map/ppermute | solution.py:210
  13.5 3.5 %collective-permute-start.5 = (bf16[1,272,128]{2,1,0:T(8,128)(2,1)S(1)}, bf16[1,272,128]{2,1,0:T(8,128)(2,1)S(1)}, u32[]{:S(2)}, u32[]{:S(2)}) collective-permute-start(bf16[1,272,128]{2,1,0:T(8,128)(2,1)S(1)} %collective-permute-done.1.refs_2_), channel_id=1, source_target_pairs={{0,2},{1,3},{2,0},{3,1},{4,6},{5,7},{6,4},{7,5},{8,10},{9,11},{10,... | collective-permute-start | bytes 208904 | tf_op jit(solution)/shard_map/ppermute | solution.py:210
  18.0 6.9 %collective-permute-start.7 = (bf16[3,272,128]{2,1,0:T(8,128)(2,1)S(1)}, bf16[3,272,128]{2,1,0:T(8,128)(2,1)S(1)}, u32[]{:S(2)}, u32[]{:S(2)}) collective-permute-start(bf16[3,272,128]{2,1,0:T(8,128)(2,1)S(1)} %get-tuple-element.18.refs_2_), channel_id=1, source_target_pairs={{0,1},{1,0},{2,3},{3,2},{4,5},{5,4},{6,7},{7,6},{8,9},{9,8},{10,11... | collective-permute-start | bytes 626696 | tf_op jit(solution)/shard_map/ppermute | solution.py:210
  19.5 3.7 %collective-permute-start.8 = (bf16[1,272,128]{2,1,0:T(8,128)(2,1)S(1)}, bf16[1,272,128]{2,1,0:T(8,128)(2,1)S(1)}, u32[]{:S(2)}, u32[]{:S(2)}) collective-permute-start(bf16[1,272,128]{2,1,0:T(8,128)(2,1)S(1)} %collective-permute-done.3.refs_0_), channel_id=1, source_target_pairs={{0,2},{1,3},{2,0},{3,1},{4,6},{5,7},{6,4},{7,5},{8,10},{9,11},{10,... | collective-permute-start | bytes 208904 | tf_op jit(solution)/shard_map/ppermute | solution.py:210
  23.1 2.6 %collective-permute-start.9 = (bf16[1,272,128]{2,1,0:T(8,128)(2,1)S(1)}, bf16[1,272,128]{2,1,0:T(8,128)(2,1)S(1)}, u32[]{:S(2)}, u32[]{:S(2)}) collective-permute-start(bf16[1,272,128]{2,1,0:T(8,128)(2,1)S(1)} %collective-permute-done.8.refs_1_.refs_3_), channel_id=1, source_target_pairs={{0,1},{1,0},{2,3},{3,2},{4,5},{5,4},{6,7},{7,6},{8,9},{9,8},{10,11... | collective-permute-start | bytes 208904 | tf_op jit(solution)/shard_map/ppermute | solution.py:210

commit v2 on v1

--- a/solution.py
+++ b/solution.py
@@ -24,13 +24,13 @@
 VMEM = pl.BlockSpec(memory_space=pltpu.VMEM)
 
 
-def call(kernel, out_shape, operands, scratch=(), flops=0):
+def call(kernel, out_shape, operands, scratch=(), flops=0, out_spec=VMEM):
     size = sum(x.size * x.dtype.itemsize for x in operands)
     return pl.pallas_call(
         kernel,
         out_shape=out_shape,
         in_specs=[VMEM] * len(operands),
-        out_specs=jax.tree.map(lambda s: VMEM, out_shape),
+        out_specs=jax.tree.map(lambda s: out_spec, out_shape),
         scratch_shapes=scratch,
         compiler_params=pltpu.CompilerParams(vmem_limit_bytes=vmem_bytes),
         cost_estimate=pl.CostEstimate(flops=flops, bytes_accessed=size, transcendentals=0),
@@ -105,12 +105,12 @@
     return total
 
 
-def accumulate(qs_ref, query_pos, before, after, pieces):
+def accumulate(qs_ref, query_pos, before, after, pieces, groups=None):
     stack = 4 if HEADS % 4 == 0 else 1
     tokens = query_pos.shape[0]
     span = stack * tokens
     small = sum(p.shape[0] for p in pieces) <= 8
-    for r in range(HEADS // stack):
+    for r in groups or range(HEADS // stack):
         at = slice(r * span, (r + 1) * span)
         start = None if before is None else before[at, :]
         if small:
@@ -154,25 +154,36 @@
 
 
 def last_kernel(count, qs_ref, qpos_ref, before_ref, *refs):
-    pieces = refs[:count]
-    o_ref, acc_ref = refs[count:]
+    pieces = refs[:-4]
+    o_ref, acc_ref, out_ref, sems = refs[-4:]
     query_pos = qpos_ref[...]
     tokens = query_pos.shape[0]
     scale = HEAD_DIM ** (-0.5)
-    accumulate(qs_ref, query_pos, before_ref, acc_ref, pieces[:1])
-
-    def store():
-        for h in range(HEADS):
+    stack = 4 if HEADS % 4 == 0 else 1
+
+    def copy(r):
+        at = slice(r * stack * HEAD_DIM, (r + 1) * stack * HEAD_DIM)
+        return pltpu.make_async_copy(out_ref.at[:, at], o_ref.at[:, at], sems.at[r])
+
+    def divide(r):
+        for h in range(r * stack, (r + 1) * stack):
             part = acc_ref[h * tokens : (h + 1) * tokens, :]
-            o_ref[:, h * HEAD_DIM : (h + 1) * HEAD_DIM] = (
+            out_ref[:, h * HEAD_DIM : (h + 1) * HEAD_DIM] = (
                 part[:, :HEAD_DIM] / part[:, HEAD_DIM:]
-            ).astype(o_ref.dtype)
-
-    store()
+            ).astype(out_ref.dtype)
+
+    groups = range(HEADS // stack)
+    for r in groups:
+        accumulate(qs_ref, query_pos, before_ref, acc_ref, pieces[:count], (r,))
+        divide(r)
+        copy(r).start()
     den = acc_ref[:, HEAD_DIM:]
     good = (den >= den_low) & (den <= den_high)
-
-    @pl.when(jnp.min(jnp.where(good, 1.0, 0.0)) < 0.5)
+    worst = jnp.min(jnp.where(good, 1.0, 0.0))
+    for r in groups:
+        copy(r).wait()
+
+    @pl.when(worst < 0.5)
     def _():
         def one_head(h, carry):
             at = pl.ds(pl.multiple_of(h * tokens, tokens), tokens)
@@ -203,7 +214,11 @@
             return carry
 
         lax.fori_loop(0, HEADS, one_head, 0)
-        store()
+        for r in groups:
+            divide(r)
+            copy(r).start()
+        for r in groups:
+            copy(r).wait()
 
 
 def swap(x, axis, size, bit):
@@ -256,17 +271,23 @@
     )
     xz3 = swap(z3, "cols", cols, 2)
     cb1 = swap(b1, "cols", cols, 1)
-    acc2, b2 = further(acc1, [z3, xz2, xz1], True)
+    acc2, b2 = further(acc1, [z3, xz2], True)
     cb2 = swap(b2, "cols", cols, 1)
+    cx1 = swap(xz1, "cols", cols, 1)
     (acc3,) = further(acc2, [cb1], False)
     c3 = swap(xz3, "cols", cols, 1)
-    (acc4,) = further(acc3, [cb2, xz3], False)
-    pieces = [c3, b1, b2, xz3, cb1, cb2]
+    (acc4,) = further(acc3, [cb2, cx1, xz1], False)
+    pieces = [xz3, c3, b1, b2, xz1, cb1, cb2, cx1]
     return call(
-        functools.partial(last_kernel, len(pieces)),
+        functools.partial(last_kernel, 2),
         jax.ShapeDtypeStruct(queries.shape, jnp.bfloat16),
         [qs, query_pos, acc4, *pieces],
-        scratch=[pltpu.VMEM(acc.shape, acc.dtype)], flops=work([c3]),
+        scratch=[
+            pltpu.VMEM(acc.shape, acc.dtype),
+            pltpu.VMEM(queries.shape, jnp.bfloat16),
+            pltpu.SemaphoreType.DMA((HEADS,)),
+        ],
+        flops=work([c3]), out_spec=pl.BlockSpec(memory_space=pltpu.HBM),
     )
 
 

time: 95.1 us -> 89 us (0.936)
  Pallas kernels: 73.8 us -> 68.7 us
  waiting for transfers between devices: 8.02 us -> 6.19 us
    pallas_call x6, Pallas kernels: 73.8 us -> 68.7 us  [call(): pl.pallas_call(kernel, out_shape=out_shape, in_specs=[VMEM] * len(operand...]
    ppermute x10 -> x11, waiting for transfers between devices: 8.02 us -> 6.19 us  [swap(): return lax.ppermute(x, axis, [(i, i ^ bit) for i in range(size)])]
    ppermute x10 -> x11, starting transfers between devices: 13.1 us -> 13.8 us  [swap(): return lax.ppermute(x, axis, [(i, i ^ bit) for i in range(size)])]
  transfers between devices with their start and end apart: 10 -> 11, of which waited for: 5 -> 4; matrix products, arithmetic and copies ran while one was open for 0% -> 0% of each run, Pallas kernels for 3% -> 2%
where the time goes in v2:
time: 89 us; the launch traced here: 88.8 us
  Pallas kernels  68.7 us (77%)
  starting transfers between devices  13.8 us (16%)
  waiting for transfers between devices  6.19 us (7%)
    pallas_call x6, Pallas kernels, call(): pl.pallas_call(kernel, out_shape=out_shape, in_specs=[VMEM] * len(operand...  68.7 us
    ppermute x11, starting transfers between devices, swap(): return lax.ppermute(x, axis, [(i, i ^ bit) for i in range(size)])  13.8 us
    ppermute x11, waiting for transfers between devices, swap(): return lax.ppermute(x, axis, [(i, i ^ bit) for i in range(size)])  6.19 us
  transfers between devices with their start and end apart: 11, of which 4 were waited for; matrix products, arithmetic and copies ran while one was open for 0% of the time, Pallas kernels for 2%

profile of v2, /device:TPU:1, one launch (start us, length us, event | category | flops | bytes accessed | tf_op | source)
XLA Modules:
  0.0 88.8 jit_solution(13517254313850333110)
XLA Ops:
  0.0 1.1 %shard_map.46 = (bf16[1,272,128]{2,1,0:T(8,128)(2,1)S(1)}, bf16[1024,128]{1,0:T(8,128)(2,1)S(1)}) custom-call(bf16[128,128]{1,0:T(8,128)(2,1)} %key_ref.1, bf16[128,128]{1,0:T(8,128)(2,1)} %value_ref.1, s32[1,128]{1,0:T(1,128)} %bitcast.1, bf16[128,1024]{1,0:T(8,128)(2,1)} %q_ref.1), custom_call_target="tpu_custom_call" | custom-call | bytes 328192 | tf_op jit(solution)/shard_map/pallas_call | solution.py:29
  1.1 0.0 copy-start
  1.1 3.2 %collective-permute-start = (bf16[1,272,128]{2,1,0:T(8,128)(2,1)S(1)}, bf16[1,272,128]{2,1,0:T(8,128)(2,1)S(1)}, u32[]{:S(2)}, u32[]{:S(2)}) collective-permute-start(bf16[1,272,128]{2,1,0:T(8,128)(2,1)S(1)} %get-tuple-element.13.refs_0_), channel_id=1, source_target_pairs={{0,8},{4,12},{8,0},{12,4},{1,9},{5,13},{9,1},{13,5},{2,10},{6,14},... | collective-permute-start | bytes 208904 | tf_op jit(solution)/shard_map/ppermute | solution.py:225
  4.3 1.3 %collective-permute-start.1 = (bf16[1,272,128]{2,1,0:T(8,128)(2,1)S(1)}, bf16[1,272,128]{2,1,0:T(8,128)(2,1)S(1)}, u32[]{:S(2)}, u32[]{:S(2)}) collective-permute-start(bf16[1,272,128]{2,1,0:T(8,128)(2,1)S(1)} %get-tuple-element.13.refs_0_), channel_id=1, source_target_pairs={{0,4},{4,0},{8,12},{12,8},{1,5},{5,1},{9,13},{13,9},{2,6},{6,2},{1... | collective-permute-start | bytes 208904 | tf_op jit(solution)/shard_map/ppermute | solution.py:225
  5.6 1.2 %collective-permute-start.2 = (bf16[1,272,128]{2,1,0:T(8,128)(2,1)S(1)}, bf16[1,272,128]{2,1,0:T(8,128)(2,1)S(1)}, u32[]{:S(2)}, u32[]{:S(2)}) collective-permute-start(bf16[1,272,128]{2,1,0:T(8,128)(2,1)S(1)} %get-tuple-element.13.refs_0_), channel_id=1, source_target_pairs={{0,2},{1,3},{2,0},{3,1},{4,6},{5,7},{6,4},{7,5},{8,10},{9,11},{10,... | collective-permute-start | bytes 208904 | tf_op jit(solution)/shard_map/ppermute | solution.py:225
  6.8 0.0 collective-permute-done.refs_1_
  6.8 1.2 %collective-permute-done.1.refs_2_ = bf16[1,272,128]{2,1,0:T(8,128)(2,1)S(1)} collective-permute-done((bf16[1,272,128]{2,1,0:T(8,128)(2,1)S(1)}, bf16[1,272,128]{2,1,0:T(8,128)(2,1)S(1)}, u32[]{:S(2)}, u32[]{:S(2)}) %collective-permute-start.1) | collective-permute-done | bytes 69664 | tf_op jit(solution)/shard_map/ppermute | solution.py:225
  8.0 1.0 %collective-permute-done.2.refs_3_ = bf16[1,272,128]{2,1,0:T(8,128)(2,1)S(1)} collective-permute-done((bf16[1,272,128]{2,1,0:T(8,128)(2,1)S(1)}, bf16[1,272,128]{2,1,0:T(8,128)(2,1)S(1)}, u32[]{:S(2)}, u32[]{:S(2)}) %collective-permute-start.2) | collective-permute-done | bytes 69664 | tf_op jit(solution)/shard_map/ppermute | solution.py:225
  9.0 0.0 copy-done
  9.0 1.0 %shard_map.47 = (f32[1024,256]{1,0:T(8,128)S(1)}, bf16[4,272,128]{2,1,0:T(8,128)(2,1)S(1)}, f32[128,128]{1,0:T(8,128)S(1)}) custom-call(bf16[1024,128]{1,0:T(8,128)(2,1)S(1)} %get-tuple-element.12.qs_ref, s32[1,128]{1,0:T(1,128)S(1)} %bitcast.2, bf16[1,272,128]{2,1,0:T(8,128)(2,1)S(1)} %get-tuple-element.13.refs_0_, ...), custom_call_target="tpu_custom_call" | custom-call | flops 268435456 | bytes 541184 | tf_op jit(solution)/shard_map/pallas_call | solution.py:29
  10.0 2.2 %collective-permute-start.5 = (bf16[4,272,128]{2,1,0:T(8,128)(2,1)S(1)}, bf16[4,272,128]{2,1,0:T(8,128)(2,1)S(1)}, u32[]{:S(2)}, u32[]{:S(2)}) collective-permute-start(bf16[4,272,128]{2,1,0:T(8,128)(2,1)S(1)} %get-tuple-element.17.refs_2_), channel_id=1, source_target_pairs={{0,1},{1,0},{2,3},{3,2},{4,5},{5,4},{6,7},{7,6},{8,9},{9,8},{10,11... | collective-permute-start | bytes 835592 | tf_op jit(solution)/shard_map/ppermute | solution.py:225
  12.1 0.2 collective-permute-start.3
  12.3 1.2 %collective-permute-start.4 = (bf16[1,272,128]{2,1,0:T(8,128)(2,1)S(1)}, bf16[1,272,128]{2,1,0:T(8,128)(2,1)S(1)}, u32[]{:S(2)}, u32[]{:S(2)}) collective-permute-start(bf16[1,272,128]{2,1,0:T(8,128)(2,1)S(1)} %collective-permute-done.refs_1_), channel_id=1, source_target_pairs={{0,2},{1,3},{2,0},{3,1},{4,6},{5,7},{6,4},{7,5},{8,10},{9,11},{10,... | collective-permute-start | bytes 208904 | tf_op jit(solution)/shard_map/ppermute | solution.py:225
  13.5 0.2 collective-permute-start.7
  13.8 2.0 %collective-permute-done.3.refs_0_ = bf16[1,272,128]{2,1,0:T(8,128)(2,1)S(1)} collective-permute-done((bf16[1,272,128]{2,1,0:T(8,128)(2,1)S(1)}, bf16[1,272,128]{2,1,0:T(8,128)(2,1)S(1)}, u32[]{:S(2)}, u32[]{:S(2)}) %collective-permute-start.3) | collective-permute-done | bytes 69664 | tf_op jit(solution)/shard_map/ppermute | solution.py:225
  15.8 0.0 collective-permute-done.4.refs_1_
  15.8 0.6 shard_map.48
  16.4 1.6 %collective-permute-start.6 = (bf16[2,272,128]{2,1,0:T(8,128)(2,1)S(1)}, bf16[2,272,128]{2,1,0:T(8,128)(2,1)S(1)}, u32[]{:S(2)}, u32[]{:S(2)}) collective-permute-start(bf16[2,272,128]{2,1,0:T(8,128)(2,1)S(1)} %get-tuple-element.18.refs_3_), channel_id=1, source_target_pairs={{0,1},{1,0},{2,3},{3,2},{4,5},{5,4},{6,7},{7,6},{8,9},{9,8},{10,11... | collective-permute-start | bytes 417800 | tf_op jit(solution)/shard_map/ppermute | solution.py:225
  18.0 1.5 %collective-permute-start.9 = (bf16[1,272,128]{2,1,0:T(8,128)(2,1)S(1)}, bf16[1,272,128]{2,1,0:T(8,128)(2,1)S(1)}, u32[]{:S(2)}, u32[]{:S(2)}) collective-permute-start(bf16[1,272,128]{2,1,0:T(8,128)(2,1)S(1)} %collective-permute-done.3.refs_0_), channel_id=1, source_target_pairs={{0,2},{1,3},{2,0},{3,1},{4,6},{5,7},{6,4},{7,5},{8,10},{9,11},{10,... | collective-permute-start | bytes 208904 | tf_op jit(solution)/shard_map/ppermute | solution.py:225
  19.5 0.0 collective-permute-done.7.refs_2_.refs_4_
  19.5 0.4 collective-permute-start.8
  19.9 1.9 %collective-permute-done.9.refs_0_ = bf16[1,272,128]{2,1,0:T(8,128)(2,1)S(1)} collective-permute-done((bf16[1,272,128]{2,1,0:T(8,128)(2,1)S(1)}, bf16[1,272,128]{2,1,0:T(8,128)(2,1)S(1)}, u32[]{:S(2)}, u32[]{:S(2)}) %collective-permute-start.9) | collective-permute-done | bytes 69664 | tf_op jit(solution)/shard_map/ppermute | solution.py:225
  21.8 0.9 collective-permute-start.10
  22.6 0.0 collective-permute-done.5.refs_0_.refs_5_
  22.6 0.8 shard_map.49.before_ref
  23.5 0.0 collective-permute-done.8.refs_1_.refs_7_
  23.5 0.0 collective-permute-done.6.refs_0_.refs_6_
  23.5 0.8 shard_map.50.before_ref
  24.3 0.0 collective-permute-done.10.refs_1_
  24.3 64.5 %shard_map.51 = bf16[128,1024]{1,0:T(8,128)(2,1)} custom-call(bf16[1024,128]{1,0:T(8,128)(2,1)S(1)} %get-tuple-element.12.qs_ref, f32[128,128]{1,0:T(8,128)S(1)} %get-tuple-element.14.qpos_ref, f32[1024,256]{1,0:T(8,128)S(1)} %shard_map.50.before_ref, bf16[1,272,128]{2,1,0:T(8,128)(2,1)S(1)} %collective-permute-done.9.refs_0_, ...), custom_call_target="tpu_custom_call" | custom-call | flops 67108864 | bytes 2490368 | tf_op jit(solution)/shard_map/pallas_call | solution.py:29
Async XLA Ops:
  1.1 8.0 %copy-start = (s32[128]{0:T(128)S(1)}, s32[128]{0:T(128)}, u32[]{:S(2)}) copy-start(s32[128]{0:T(128)} %param.7) | copy-start | bytes 1540
  1.1 5.7 %collective-permute-start = (bf16[1,272,128]{2,1,0:T(8,128)(2,1)S(1)}, bf16[1,272,128]{2,1,0:T(8,128)(2,1)S(1)}, u32[]{:S(2)}, u32[]{:S(2)}) collective-permute-start(bf16[1,272,128]{2,1,0:T(8,128)(2,1)S(1)} %get-tuple-element.13.refs_0_), channel_id=1, source_target_pairs={{0,8},{4,12},{8,0},{12,4},{1,9},{5,13},{9,1},{13,5},{2,10},{6,14},... | collective-permute-start | bytes 208904 | tf_op jit(solution)/shard_map/ppermute | solution.py:225
  4.3 3.7 %collective-permute-start.1 = (bf16[1,272,128]{2,1,0:T(8,128)(2,1)S(1)}, bf16[1,272,128]{2,1,0:T(8,128)(2,1)S(1)}, u32[]{:S(2)}, u32[]{:S(2)}) collective-permute-start(bf16[1,272,128]{2,1,0:T(8,128)(2,1)S(1)} %get-tuple-element.13.refs_0_), channel_id=1, source_target_pairs={{0,4},{4,0},{8,12},{12,8},{1,5},{5,1},{9,13},{13,9},{2,6},{6,2},{1... | collective-permute-start | bytes 208904 | tf_op jit(solution)/shard_map/ppermute | solution.py:225
  5.6 3.5 %collective-permute-start.2 = (bf16[1,272,128]{2,1,0:T(8,128)(2,1)S(1)}, bf16[1,272,128]{2,1,0:T(8,128)(2,1)S(1)}, u32[]{:S(2)}, u32[]{:S(2)}) collective-permute-start(bf16[1,272,128]{2,1,0:T(8,128)(2,1)S(1)} %get-tuple-element.13.refs_0_), channel_id=1, source_target_pairs={{0,2},{1,3},{2,0},{3,1},{4,6},{5,7},{6,4},{7,5},{8,10},{9,11},{10,... | collective-permute-start | bytes 208904 | tf_op jit(solution)/shard_map/ppermute | solution.py:225
  10.0 12.6 %collective-permute-start.5 = (bf16[4,272,128]{2,1,0:T(8,128)(2,1)S(1)}, bf16[4,272,128]{2,1,0:T(8,128)(2,1)S(1)}, u32[]{:S(2)}, u32[]{:S(2)}) collective-permute-start(bf16[4,272,128]{2,1,0:T(8,128)(2,1)S(1)} %get-tuple-element.17.refs_2_), channel_id=1, source_target_pairs={{0,1},{1,0},{2,3},{3,2},{4,5},{5,4},{6,7},{7,6},{8,9},{9,8},{10,11... | collective-permute-start | bytes 835592 | tf_op jit(solution)/shard_map/ppermute | solution.py:225
  12.1 3.7 %collective-permute-start.3 = (bf16[1,272,128]{2,1,0:T(8,128)(2,1)S(1)}, bf16[1,272,128]{2,1,0:T(8,128)(2,1)S(1)}, u32[]{:S(2)}, u32[]{:S(2)}) collective-permute-start(bf16[1,272,128]{2,1,0:T(8,128)(2,1)S(1)} %collective-permute-done.refs_1_), channel_id=1, source_target_pairs={{0,4},{4,0},{8,12},{12,8},{1,5},{5,1},{9,13},{13,9},{2,6},{6,2},{1... | collective-permute-start | bytes 208904 | tf_op jit(solution)/shard_map/ppermute | solution.py:225
  12.3 3.5 %collective-permute-start.4 = (bf16[1,272,128]{2,1,0:T(8,128)(2,1)S(1)}, bf16[1,272,128]{2,1,0:T(8,128)(2,1)S(1)}, u32[]{:S(2)}, u32[]{:S(2)}) collective-permute-start(bf16[1,272,128]{2,1,0:T(8,128)(2,1)S(1)} %collective-permute-done.refs_1_), channel_id=1, source_target_pairs={{0,2},{1,3},{2,0},{3,1},{4,6},{5,7},{6,4},{7,5},{8,10},{9,11},{10,... | collective-permute-start | bytes 208904 | tf_op jit(solution)/shard_map/ppermute | solution.py:225
  13.5 6.0 %collective-permute-start.7 = (bf16[1,272,128]{2,1,0:T(8,128)(2,1)S(1)}, bf16[1,272,128]{2,1,0:T(8,128)(2,1)S(1)}, u32[]{:S(2)}, u32[]{:S(2)}) collective-permute-start(bf16[1,272,128]{2,1,0:T(8,128)(2,1)S(1)} %collective-permute-done.1.refs_2_), channel_id=1, source_target_pairs={{0,2},{1,3},{2,0},{3,1},{4,6},{5,7},{6,4},{7,5},{8,10},{9,11},{10,... | collective-permute-start | bytes 208904 | tf_op jit(solution)/shard_map/ppermute | solution.py:225
  16.4 7.1 %collective-permute-start.6 = (bf16[2,272,128]{2,1,0:T(8,128)(2,1)S(1)}, bf16[2,272,128]{2,1,0:T(8,128)(2,1)S(1)}, u32[]{:S(2)}, u32[]{:S(2)}) collective-permute-start(bf16[2,272,128]{2,1,0:T(8,128)(2,1)S(1)} %get-tuple-element.18.refs_3_), channel_id=1, source_target_pairs={{0,1},{1,0},{2,3},{3,2},{4,5},{5,4},{6,7},{7,6},{8,9},{9,8},{10,11... | collective-permute-start | bytes 417800 | tf_op jit(solution)/shard_map/ppermute | solution.py:225
  18.0 3.8 %collective-permute-start.9 = (bf16[1,272,128]{2,1,0:T(8,128)(2,1)S(1)}, bf16[1,272,128]{2,1,0:T(8,128)(2,1)S(1)}, u32[]{:S(2)}, u32[]{:S(2)}) collective-permute-start(bf16[1,272,128]{2,1,0:T(8,128)(2,1)S(1)} %collective-permute-done.3.refs_0_), channel_id=1, source_target_pairs={{0,2},{1,3},{2,0},{3,1},{4,6},{5,7},{6,4},{7,5},{8,10},{9,11},{10,... | collective-permute-start | bytes 208904 | tf_op jit(solution)/shard_map/ppermute | solution.py:225
  19.5 4.0 %collective-permute-start.8 = (bf16[1,272,128]{2,1,0:T(8,128)(2,1)S(1)}, bf16[1,272,128]{2,1,0:T(8,128)(2,1)S(1)}, u32[]{:S(2)}, u32[]{:S(2)}) collective-permute-start(bf16[1,272,128]{2,1,0:T(8,128)(2,1)S(1)} %collective-permute-done.7.refs_2_.refs_4_), channel_id=1, source_target_pairs={{0,1},{1,0},{2,3},{3,2},{4,5},{5,4},{6,7},{7,6},{8,9},{9,8},{10,11... | collective-permute-start | bytes 208904 | tf_op jit(solution)/shard_map/ppermute | solution.py:225
  21.8 2.5 %collective-permute-start.10 = (bf16[1,272,128]{2,1,0:T(8,128)(2,1)S(1)}, bf16[1,272,128]{2,1,0:T(8,128)(2,1)S(1)}, u32[]{:S(2)}, u32[]{:S(2)}) collective-permute-start(bf16[1,272,128]{2,1,0:T(8,128)(2,1)S(1)} %collective-permute-done.9.refs_0_), channel_id=1, source_target_pairs={{0,1},{1,0},{2,3},{3,2},{4,5},{5,4},{6,7},{7,6},{8,9},{9,8},{10,11... | collective-permute-start | bytes 208904 | tf_op jit(solution)/shard_map/ppermute | solution.py:225

commit v3 on v2

--- a/solution.py
+++ b/solution.py
@@ -37,8 +37,9 @@
     )(*operands)
 
 
-def pack_kernel(key_ref, value_ref, pos_ref, q_ref, block_ref, qs_ref):
+def pack_kernel(key_ref, value_ref, pos_ref, block_ref, near_pos_ref):
     tokens = key_ref.shape[0]
+    near_pos_ref[...] = pos_ref[...].astype(jnp.float32)
     block_ref[0, :tokens, :] = key_ref[...]
     block_ref[0, tokens : 2 * tokens, :] = value_ref[...]
     row = lax.broadcasted_iota(jnp.int32, (POS_ROWS, LANES), 0)
@@ -50,8 +51,6 @@
         tile = jnp.where(row == 2 * j, jnp.broadcast_to(high, tile.shape), tile)
         tile = jnp.where(row == 2 * j + 1, jnp.broadcast_to(low, tile.shape), tile)
     block_ref[0, 2 * tokens :, :] = tile.astype(block_ref.dtype)
-    for h in range(HEADS):
-        qs_ref[h * tokens : (h + 1) * tokens, :] = q_ref[:, h * HEAD_DIM : (h + 1) * HEAD_DIM]
 
 
 def block_rows(ref):
@@ -135,22 +134,24 @@
         at += p.shape[0]
 
 
-def first_kernel(count, qs_ref, pos_ref, *refs):
-    pieces = refs[:count]
-    acc_ref, bundle_ref, qpos_ref = refs[count:]
+def bundle_kernel(groups, *refs):
+    for group, out_ref in zip(groups, refs[-len(groups) :]):
+        bundle([refs[i] for i in group], out_ref)
+
+
+def first_kernel(count, q_ref, pos_ref, *refs):
+    acc_ref, qpos_ref, qs_ref = refs[count:]
     tokens = pos_ref.shape[1]
-    bundle(pieces, bundle_ref)
+    for h in range(HEADS):
+        qs_ref[h * tokens : (h + 1) * tokens, :] = q_ref[:, h * HEAD_DIM : (h + 1) * HEAD_DIM]
     qpos_ref[...] = jnp.transpose(
-        jnp.broadcast_to(pos_ref[...].astype(jnp.float32), (LANES, tokens))
-    )
-    accumulate(qs_ref, qpos_ref[...], None, acc_ref, pieces)
+        jnp.broadcast_to(pos_ref[...], (LANES, tokens))
+    )
+    accumulate(qs_ref, qpos_ref[...], None, acc_ref, refs[:count])
 
 
 def next_kernel(count, qs_ref, qpos_ref, before_ref, *refs):
-    pieces = refs[:count]
-    if len(refs) > count + 1:
-        bundle(pieces, refs[count + 1])
-    accumulate(qs_ref, qpos_ref[...], before_ref, refs[count], pieces)
+    accumulate(qs_ref, qpos_ref[...], before_ref, refs[count], refs[:count])
 
 
 def last_kernel(count, qs_ref, qpos_ref, before_ref, *refs):
@@ -221,6 +222,13 @@
             copy(r).wait()
 
 
+def hop(x, rows, cols, row_bit, col_bit):
+    pairs = [
+        (r * cols + c, (r ^ row_bit) * cols + (c ^ col_bit)) for r in range(rows) for c in range(cols)
+    ]
+    return lax.ppermute(x, ("rows", "cols"), pairs)
+
+
 def swap(x, axis, size, bit):
     return lax.ppermute(x, axis, [(i, i ^ bit) for i in range(size)])
 
@@ -230,26 +238,33 @@
     pos = positions.reshape(1, tokens)
     block = jax.ShapeDtypeStruct((1, 2 * tokens + POS_ROWS, HEAD_DIM), jnp.bfloat16)
     in_hbm = functools.partial(pltpu.with_memory_space_constraint, memory_space=pltpu.HBM)
-    own, qs = call(
+    own, near_pos = call(
         pack_kernel,
-        (block, jax.ShapeDtypeStruct((HEADS * tokens, HEAD_DIM), jnp.bfloat16)),
-        [in_hbm(x) for x in (keys, values, pos, queries)],
+        (
+            block,
+            jax.ShapeDtypeStruct((1, tokens), jnp.float32),
+        ),
+        [in_hbm(x) for x in (keys, values, pos)],
     )
     acc = jax.ShapeDtypeStruct((HEADS * tokens, 2 * HEAD_DIM), jnp.float32)
     qpos = jax.ShapeDtypeStruct((tokens, LANES), jnp.float32)
-
-    def bundled(pieces):
-        return jax.ShapeDtypeStruct(
-            (sum(p.shape[0] for p in pieces),) + pieces[0].shape[1:], jnp.bfloat16
+    heads = jax.ShapeDtypeStruct((HEADS * tokens, HEAD_DIM), jnp.bfloat16)
+
+    def together(pieces, *groups):
+        shapes = tuple(
+            jax.ShapeDtypeStruct(
+                (sum(pieces[i].shape[0] for i in g),) + pieces[0].shape[1:], jnp.bfloat16
+            )
+            for g in groups
         )
+        return call(functools.partial(bundle_kernel, groups), shapes, pieces)
 
     def work(pieces):
         return 4 * HEADS * tokens * HEAD_DIM * tokens * sum(p.shape[0] for p in pieces)
 
-    def further(before, pieces, with_bundle):
-        out = (acc, bundled(pieces)) if with_bundle else (acc,)
+    def further(before, pieces):
         return call(
-            functools.partial(next_kernel, len(pieces)), out,
+            functools.partial(next_kernel, len(pieces)), acc,
             [qs, query_pos, before, *pieces], flops=work(pieces),
         )
 
@@ -257,29 +272,25 @@
     while bit >= 4:
         own = jnp.concatenate([own, swap(own, "rows", rows, bit)], axis=0)
         bit //= 2
-    z2 = swap(own, "rows", rows, 2)
-    z1 = swap(own, "rows", rows, 1)
-    xo = swap(own, "cols", cols, 2)
-    z3 = swap(z2, "rows", rows, 1)
-    xz2 = swap(z2, "cols", cols, 2)
-    xz1 = swap(z1, "cols", cols, 2)
-    near = [own, z2, z1, xo]
-    acc1, b1, query_pos = call(
-        functools.partial(first_kernel, len(near)),
-        (acc, bundled(near), qpos),
-        [qs, pos, *near], flops=work(near),
-    )
-    xz3 = swap(z3, "cols", cols, 2)
+    z2 = hop(own, rows, cols, 2, 0)
+    z1 = hop(own, rows, cols, 1, 0)
+    xo = hop(own, rows, cols, 0, 2)
+    xz3 = hop(z2, rows, cols, 1, 2)
+    xz2 = hop(z2, rows, cols, 0, 2)
+    b12, b1 = together([own, z2, z1, xo], (1, 3), (0, 1, 2, 3))
+    zb = hop(b12, rows, cols, 1, 0)
     cb1 = swap(b1, "cols", cols, 1)
-    acc2, b2 = further(acc1, [z3, xz2], True)
+    acc1, query_pos, qs = call(
+        functools.partial(first_kernel, 1), (acc, qpos, heads), [in_hbm(queries), near_pos, b1], flops=work([b1])
+    )
+    (b2,) = together([xz3, xz2], (0, 1))
     cb2 = swap(b2, "cols", cols, 1)
-    cx1 = swap(xz1, "cols", cols, 1)
-    (acc3,) = further(acc2, [cb1], False)
-    c3 = swap(xz3, "cols", cols, 1)
-    (acc4,) = further(acc3, [cb2, cx1, xz1], False)
-    pieces = [xz3, c3, b1, b2, xz1, cb1, cb2, cx1]
+    acc2 = further(acc1, [cb1, b2])
+    czb = swap(zb, "cols", cols, 1)
+    acc4 = further(acc2, [cb2, zb])
+    pieces = [czb, b1, cb1, b2, cb2, zb]
     return call(
-        functools.partial(last_kernel, 2),
+        functools.partial(last_kernel, 1),
         jax.ShapeDtypeStruct(queries.shape, jnp.bfloat16),
         [qs, query_pos, acc4, *pieces],
         scratch=[
@@ -287,7 +298,7 @@
             pltpu.VMEM(queries.shape, jnp.bfloat16),
             pltpu.SemaphoreType.DMA((HEADS,)),
         ],
-        flops=work([c3]), out_spec=pl.BlockSpec(memory_space=pltpu.HBM),
+        flops=work([czb]), out_spec=pl.BlockSpec(memory_space=pltpu.HBM),
     )
 
 

time: 89 us -> 96.5 us (1.084)
  Pallas kernels: 68.7 us -> 77.2 us
  starting transfers between devices: 13.8 us -> 11.8 us
  waiting for transfers between devices: 6.19 us -> 7.17 us
    ppermute x11 -> x3, starting transfers between devices: 13.8 us -> 3.51 us  [swap(): return lax.ppermute(x, axis, [(i, i ^ bit) for i in range(size)])]
    pallas_call x6 -> x7, Pallas kernels: 68.7 us -> 77.2 us  [call(): pl.pallas_call(kernel, out_shape=out_shape, in_specs=[VMEM] * len(operand...]
    ppermute x0 -> x6, starting transfers between devices: none -> 8.28 us  [hop(): return lax.ppermute(x, ('rows', 'cols'), pairs)]
    ppermute x0 -> x6, waiting for transfers between devices: none -> 7.17 us  [hop(): return lax.ppermute(x, ('rows', 'cols'), pairs)]
    ppermute x11 -> x3, waiting for transfers between devices: 6.19 us -> 0.01 us  [swap(): return lax.ppermute(x, axis, [(i, i ^ bit) for i in range(size)])]
  transfers between devices with their start and end apart: 11 -> 9, of which waited for: 4 -> 3; matrix products, arithmetic and copies ran while one was open for 0% -> 0% of each run, Pallas kernels for 2% -> 4%
where the time goes in v3:
time: 96.5 us; the launch traced here: 96.3 us
  Pallas kernels  77.2 us (80%)
  starting transfers between devices  11.8 us (12%)
  waiting for transfers between devices  7.17 us (7%)
    pallas_call x7, Pallas kernels, call(): pl.pallas_call(kernel, out_shape=out_shape, in_specs=[VMEM] * len(operand...  77.2 us
    ppermute x6, starting transfers between devices, hop(): return lax.ppermute(x, ('rows', 'cols'), pairs)  8.28 us
    ppermute x6, waiting for transfers between devices, hop(): return lax.ppermute(x, ('rows', 'cols'), pairs)  7.17 us
    ppermute x3, starting transfers between devices, swap(): return lax.ppermute(x, axis, [(i, i ^ bit) for i in range(size)])  3.51 us
  transfers between devices with their start and end apart: 9, of which 3 were waited for; matrix products, arithmetic and copies ran while one was open for 0% of the time, Pallas kernels for 4%

profile of v3, /device:TPU:1, one launch (start us, length us, event | category | flops | bytes accessed | tf_op | source)
XLA Modules:
  0.0 96.3 jit_solution(11259151920300348725)
XLA Ops:
  0.0 0.8 shard_map.46
  0.8 3.1 %collective-permute-start = (bf16[1,272,128]{2,1,0:T(8,128)(2,1)S(1)}, bf16[1,272,128]{2,1,0:T(8,128)(2,1)S(1)}, u32[]{:S(2)}, u32[]{:S(2)}) collective-permute-start(bf16[1,272,128]{2,1,0:T(8,128)(2,1)S(1)} %get-tuple-element.13.refs_0_), channel_id=1, source_target_pairs={{0,8},{1,9},{2,10},{3,11},{4,12},{5,13},{6,14},{7,15},{8,0},{9,1},... | collective-permute-start | bytes 208904 | tf_op jit(solution)/shard_map/ppermute | solution.py:229
  3.9 1.3 %collective-permute-start.1 = (bf16[1,272,128]{2,1,0:T(8,128)(2,1)S(1)}, bf16[1,272,128]{2,1,0:T(8,128)(2,1)S(1)}, u32[]{:S(2)}, u32[]{:S(2)}) collective-permute-start(bf16[1,272,128]{2,1,0:T(8,128)(2,1)S(1)} %get-tuple-element.13.refs_0_), channel_id=1, source_target_pairs={{0,4},{1,5},{2,6},{3,7},{4,0},{5,1},{6,2},{7,3},{8,12},{9,13},{10,... | collective-permute-start | bytes 208904 | tf_op jit(solution)/shard_map/ppermute | solution.py:229
  5.2 1.2 %collective-permute-start.2 = (bf16[1,272,128]{2,1,0:T(8,128)(2,1)S(1)}, bf16[1,272,128]{2,1,0:T(8,128)(2,1)S(1)}, u32[]{:S(2)}, u32[]{:S(2)}) collective-permute-start(bf16[1,272,128]{2,1,0:T(8,128)(2,1)S(1)} %get-tuple-element.13.refs_0_), channel_id=1, source_target_pairs={{0,2},{1,3},{2,0},{3,1},{4,6},{5,7},{6,4},{7,5},{8,10},{9,11},{10,... | collective-permute-start | bytes 208904 | tf_op jit(solution)/shard_map/ppermute | solution.py:229
  6.4 0.0 collective-permute-done.refs_1_
  6.4 1.2 %collective-permute-done.1.refs_2_ = bf16[1,272,128]{2,1,0:T(8,128)(2,1)S(1)} collective-permute-done((bf16[1,272,128]{2,1,0:T(8,128)(2,1)S(1)}, bf16[1,272,128]{2,1,0:T(8,128)(2,1)S(1)}, u32[]{:S(2)}, u32[]{:S(2)}) %collective-permute-start.1) | collective-permute-done | bytes 69664 | tf_op jit(solution)/shard_map/ppermute | solution.py:229
  7.6 1.0 %collective-permute-done.2.refs_3_ = bf16[1,272,128]{2,1,0:T(8,128)(2,1)S(1)} collective-permute-done((bf16[1,272,128]{2,1,0:T(8,128)(2,1)S(1)}, bf16[1,272,128]{2,1,0:T(8,128)(2,1)S(1)}, u32[]{:S(2)}, u32[]{:S(2)}) %collective-permute-start.2) | collective-permute-done | bytes 69664 | tf_op jit(solution)/shard_map/ppermute | solution.py:229
  8.7 2.2 %collective-permute-start.3 = (bf16[4,272,128]{2,1,0:T(8,128)(2,1)S(1)}, bf16[4,272,128]{2,1,0:T(8,128)(2,1)S(1)}, u32[]{:S(2)}, u32[]{:S(2)}) collective-permute-start(bf16[4,272,128]{2,1,0:T(8,128)(2,1)S(1)} %get-tuple-element.14.refs_0_.refs_1_), channel_id=1, source_target_pairs={{0,1},{1,0},{2,3},{3,2},{4,5},{5,4},{6,7},{7,6},{8,9},{9,8},{10,11... | collective-permute-start | bytes 835592 | tf_op jit(solution)/shard_map/ppermute | solution.py:233
  10.9 0.2 collective-permute-start.7
  11.0 2.2 %collective-permute-start.4 = (bf16[1,272,128]{2,1,0:T(8,128)(2,1)S(1)}, bf16[1,272,128]{2,1,0:T(8,128)(2,1)S(1)}, u32[]{:S(2)}, u32[]{:S(2)}) collective-permute-start(bf16[1,272,128]{2,1,0:T(8,128)(2,1)S(1)} %collective-permute-done.refs_1_), channel_id=1, source_target_pairs={{0,6},{1,7},{2,4},{3,5},{4,2},{5,3},{6,0},{7,1},{8,14},{9,15},{10,... | collective-permute-start | bytes 208904 | tf_op jit(solution)/shard_map/ppermute | solution.py:229
  13.3 0.3 collective-permute-start.5
  13.5 4.9 %collective-permute-done.4.refs_0_ = bf16[1,272,128]{2,1,0:T(8,128)(2,1)S(1)} collective-permute-done((bf16[1,272,128]{2,1,0:T(8,128)(2,1)S(1)}, bf16[1,272,128]{2,1,0:T(8,128)(2,1)S(1)}, u32[]{:S(2)}, u32[]{:S(2)}) %collective-permute-start.4) | collective-permute-done | bytes 69664 | tf_op jit(solution)/shard_map/ppermute | solution.py:229
  18.4 0.0 collective-permute-done.5.refs_1_
  18.5 1.3 %collective-permute-start.6 = (bf16[2,272,128]{2,1,0:T(8,128)(2,1)S(1)}, bf16[2,272,128]{2,1,0:T(8,128)(2,1)S(1)}, u32[]{:S(2)}, u32[]{:S(2)}) collective-permute-start(bf16[2,272,128]{2,1,0:T(8,128)(2,1)S(1)} %shard_map.49.refs_1_.refs_3_), channel_id=1, source_target_pairs={{0,1},{1,0},{2,3},{3,2},{4,5},{5,4},{6,7},{7,6},{8,9},{9,8},{10,11... | collective-permute-start | bytes 417800 | tf_op jit(solution)/shard_map/ppermute | solution.py:233
  19.7 0.0 collective-permute-done.7.refs_1_.refs_5_
  19.7 0.1 collective-permute-start.8
  19.8 1.9 %shard_map.48 = (f32[1024,256]{1,0:T(8,128)S(1)}, f32[128,128]{1,0:T(8,128)S(1)}, bf16[1024,128]{1,0:T(8,128)(2,1)S(1)}) custom-call(bf16[128,1024]{1,0:T(8,128)(2,1)} %q_ref.1, f32[1,128]{1,0:T(1,128)S(1)} %get-tuple-element.12.pos_ref, bf16[4,272,128]{2,1,0:T(8,128)(2,1)S(1)} %get-tuple-element.14.refs_0_.refs_1_), custom_call_target="tpu_custom_call" | custom-call | flops 268435456 | bytes 541184 | tf_op jit(solution)/shard_map/pallas_call | solution.py:29
  21.7 0.0 collective-permute-done.3.refs_0_.refs_2_
  21.7 1.1 %shard_map.50.before_ref = f32[1024,256]{1,0:T(8,128)S(1)} custom-call(bf16[1024,128]{1,0:T(8,128)(2,1)S(1)} %get-tuple-element.15.qs_ref, f32[128,128]{1,0:T(8,128)S(1)} %get-tuple-element.16.qpos_ref, f32[1024,256]{1,0:T(8,128)S(1)} %get-tuple-element.17.before_ref, bf16[4,272,128]{2,1,0:T(8,128)(2,1)S(1)} %collective-permute-done.3.refs_0_.refs_2_, ...), custom_call_target="tpu_custom_call" | custom-call | flops 402653184 | bytes 1794048 | tf_op jit(solution)/shard_map/pallas_call | solution.py:29
  22.9 0.0 collective-permute-done.6.refs_0_.refs_4_
  22.9 0.8 shard_map.51.before_ref
  23.7 0.0 collective-permute-done.8.refs_0_
  23.7 72.6 %shard_map.52 = bf16[128,1024]{1,0:T(8,128)(2,1)} custom-call(bf16[1024,128]{1,0:T(8,128)(2,1)S(1)} %get-tuple-element.15.qs_ref, f32[128,128]{1,0:T(8,128)S(1)} %get-tuple-element.16.qpos_ref, f32[1024,256]{1,0:T(8,128)S(1)} %shard_map.51.before_ref, bf16[2,272,128]{2,1,0:T(8,128)(2,1)S(1)} %collective-permute-done.8.refs_0_, ...), custom_call_target="tpu_custom_call" | custom-call | flops 134217728 | bytes 2490368 | tf_op jit(solution)/shard_map/pallas_call | solution.py:29
  (2 shorter events, 0.1 us)
Async XLA Ops:
  0.8 5.6 %collective-permute-start = (bf16[1,272,128]{2,1,0:T(8,128)(2,1)S(1)}, bf16[1,272,128]{2,1,0:T(8,128)(2,1)S(1)}, u32[]{:S(2)}, u32[]{:S(2)}) collective-permute-start(bf16[1,272,128]{2,1,0:T(8,128)(2,1)S(1)} %get-tuple-element.13.refs_0_), channel_id=1, source_target_pairs={{0,8},{1,9},{2,10},{3,11},{4,12},{5,13},{6,14},{7,15},{8,0},{9,1},... | collective-permute-start | bytes 208904 | tf_op jit(solution)/shard_map/ppermute | solution.py:229
  3.9 3.7 %collective-permute-start.1 = (bf16[1,272,128]{2,1,0:T(8,128)(2,1)S(1)}, bf16[1,272,128]{2,1,0:T(8,128)(2,1)S(1)}, u32[]{:S(2)}, u32[]{:S(2)}) collective-permute-start(bf16[1,272,128]{2,1,0:T(8,128)(2,1)S(1)} %get-tuple-element.13.refs_0_), channel_id=1, source_target_pairs={{0,4},{1,5},{2,6},{3,7},{4,0},{5,1},{6,2},{7,3},{8,12},{9,13},{10,... | collective-permute-start | bytes 208904 | tf_op jit(solution)/shard_map/ppermute | solution.py:229
  5.2 3.5 %collective-permute-start.2 = (bf16[1,272,128]{2,1,0:T(8,128)(2,1)S(1)}, bf16[1,272,128]{2,1,0:T(8,128)(2,1)S(1)}, u32[]{:S(2)}, u32[]{:S(2)}) collective-permute-start(bf16[1,272,128]{2,1,0:T(8,128)(2,1)S(1)} %get-tuple-element.13.refs_0_), channel_id=1, source_target_pairs={{0,2},{1,3},{2,0},{3,1},{4,6},{5,7},{6,4},{7,5},{8,10},{9,11},{10,... | collective-permute-start | bytes 208904 | tf_op jit(solution)/shard_map/ppermute | solution.py:229
  8.7 13.0 %collective-permute-start.3 = (bf16[4,272,128]{2,1,0:T(8,128)(2,1)S(1)}, bf16[4,272,128]{2,1,0:T(8,128)(2,1)S(1)}, u32[]{:S(2)}, u32[]{:S(2)}) collective-permute-start(bf16[4,272,128]{2,1,0:T(8,128)(2,1)S(1)} %get-tuple-element.14.refs_0_.refs_1_), channel_id=1, source_target_pairs={{0,1},{1,0},{2,3},{3,2},{4,5},{5,4},{6,7},{7,6},{8,9},{9,8},{10,11... | collective-permute-start | bytes 835592 | tf_op jit(solution)/shard_map/ppermute | solution.py:233
  10.9 8.9 %collective-permute-start.7 = (bf16[2,272,128]{2,1,0:T(8,128)(2,1)S(1)}, bf16[2,272,128]{2,1,0:T(8,128)(2,1)S(1)}, u32[]{:S(2)}, u32[]{:S(2)}) collective-permute-start(bf16[2,272,128]{2,1,0:T(8,128)(2,1)S(1)} %get-tuple-element.18), channel_id=1, source_target_pairs={{0,4},{1,5},{2,6},{3,7},{4,0},{5,1},{6,2},{7,3},{8,12},{9,13},{10,... | collective-permute-start | bytes 417800 | tf_op jit(solution)/shard_map/ppermute | solution.py:229
  11.0 7.4 %collective-permute-start.4 = (bf16[1,272,128]{2,1,0:T(8,128)(2,1)S(1)}, bf16[1,272,128]{2,1,0:T(8,128)(2,1)S(1)}, u32[]{:S(2)}, u32[]{:S(2)}) collective-permute-start(bf16[1,272,128]{2,1,0:T(8,128)(2,1)S(1)} %collective-permute-done.refs_1_), channel_id=1, source_target_pairs={{0,6},{1,7},{2,4},{3,5},{4,2},{5,3},{6,0},{7,1},{8,14},{9,15},{10,... | collective-permute-start | bytes 208904 | tf_op jit(solution)/shard_map/ppermute | solution.py:229
  13.3 5.2 %collective-permute-start.5 = (bf16[1,272,128]{2,1,0:T(8,128)(2,1)S(1)}, bf16[1,272,128]{2,1,0:T(8,128)(2,1)S(1)}, u32[]{:S(2)}, u32[]{:S(2)}) collective-permute-start(bf16[1,272,128]{2,1,0:T(8,128)(2,1)S(1)} %collective-permute-done.refs_1_), channel_id=1, source_target_pairs={{0,2},{1,3},{2,0},{3,1},{4,6},{5,7},{6,4},{7,5},{8,10},{9,11},{10,... | collective-permute-start | bytes 208904 | tf_op jit(solution)/shard_map/ppermute | solution.py:229
  18.5 4.4 %collective-permute-start.6 = (bf16[2,272,128]{2,1,0:T(8,128)(2,1)S(1)}, bf16[2,272,128]{2,1,0:T(8,128)(2,1)S(1)}, u32[]{:S(2)}, u32[]{:S(2)}) collective-permute-start(bf16[2,272,128]{2,1,0:T(8,128)(2,1)S(1)} %shard_map.49.refs_1_.refs_3_), channel_id=1, source_target_pairs={{0,1},{1,0},{2,3},{3,2},{4,5},{5,4},{6,7},{7,6},{8,9},{9,8},{10,11... | collective-permute-start | bytes 417800 | tf_op jit(solution)/shard_map/ppermute | solution.py:233
  19.7 4.0 %collective-permute-start.8 = (bf16[2,272,128]{2,1,0:T(8,128)(2,1)S(1)}, bf16[2,272,128]{2,1,0:T(8,128)(2,1)S(1)}, u32[]{:S(2)}, u32[]{:S(2)}) collective-permute-start(bf16[2,272,128]{2,1,0:T(8,128)(2,1)S(1)} %collective-permute-done.7.refs_1_.refs_5_), channel_id=1, source_target_pairs={{0,1},{1,0},{2,3},{3,2},{4,5},{5,4},{6,7},{7,6},{8,9},{9,8},{10,11... | collective-permute-start | bytes 417800 | tf_op jit(solution)/shard_map/ppermute | solution.py:233

commit v4 on v3

--- a/solution.py
+++ b/solution.py
@@ -276,19 +276,21 @@
     z1 = hop(own, rows, cols, 1, 0)
     xo = hop(own, rows, cols, 0, 2)
     xz3 = hop(z2, rows, cols, 1, 2)
-    xz2 = hop(z2, rows, cols, 0, 2)
-    b12, b1 = together([own, z2, z1, xo], (1, 3), (0, 1, 2, 3))
-    zb = hop(b12, rows, cols, 1, 0)
+    (b12,) = together([z2, z1], (0, 1))
+    zb = hop(b12, rows, cols, 0, 2)
+    z3 = hop(z2, rows, cols, 1, 0)
+    (b1,) = together([own, z2, z1, xo], (0, 1, 2, 3))
     cb1 = swap(b1, "cols", cols, 1)
     acc1, query_pos, qs = call(
-        functools.partial(first_kernel, 1), (acc, qpos, heads), [in_hbm(queries), near_pos, b1], flops=work([b1])
-    )
-    (b2,) = together([xz3, xz2], (0, 1))
-    cb2 = swap(b2, "cols", cols, 1)
-    acc2 = further(acc1, [cb1, b2])
+        functools.partial(first_kernel, 1), (acc, qpos, heads), [queries, near_pos, b1], flops=work([b1])
+    )
+    cc = swap(xz3, "cols", cols, 1)
+    acc2 = further(acc1, [cb1])
+    cz3 = swap(z3, "cols", cols, 1)
     czb = swap(zb, "cols", cols, 1)
-    acc4 = further(acc2, [cb2, zb])
-    pieces = [czb, b1, cb1, b2, cb2, zb]
+    acc3 = further(acc2, [zb, xz3, cc])
+    acc4 = further(acc3, [z3, cz3])
+    pieces = [czb, b1, cb1, xz3, cc, zb, z3, cz3]
     return call(
         functools.partial(last_kernel, 1),
         jax.ShapeDtypeStruct(queries.shape, jnp.bfloat16),
@@ -298,7 +300,7 @@
             pltpu.VMEM(queries.shape, jnp.bfloat16),
             pltpu.SemaphoreType.DMA((HEADS,)),
         ],
-        flops=work([czb]), out_spec=pl.BlockSpec(memory_space=pltpu.HBM),
+        flops=work([pieces[0]]), out_spec=pl.BlockSpec(memory_space=pltpu.HBM),
     )
 
 

time: 96.5 us -> 84.2 us (0.87)
  Pallas kernels: 77.2 us -> 65.8 us
  waiting for transfers between devices: 7.17 us -> 5.94 us
    pallas_call x7 -> x8, Pallas kernels: 77.2 us -> 65.8 us  [call(): pl.pallas_call(kernel, out_shape=out_shape, in_specs=[VMEM] * len(operand...]
    ppermute x6, waiting for transfers between devices: 7.17 us -> 5.93 us  [hop(): return lax.ppermute(x, ('rows', 'cols'), pairs)]
    ppermute x3 -> x4, starting transfers between devices: 3.51 us -> 3.92 us  [swap(): return lax.ppermute(x, axis, [(i, i ^ bit) for i in range(size)])]
  transfers between devices with their start and end apart: 9 -> 10, of which waited for: 3 -> 3; matrix products, arithmetic and copies ran while one was open for 0% -> 0% of each run, Pallas kernels for 4% -> 4%
where the time goes in v4:
time: 84.2 us; the launch traced here: 84.1 us
  Pallas kernels  65.8 us (78%)
  starting transfers between devices  12.3 us (15%)
  waiting for transfers between devices  5.94 us (7%)
    pallas_call x8, Pallas kernels, call(): pl.pallas_call(kernel, out_shape=out_shape, in_specs=[VMEM] * len(operand...  65.8 us
    ppermute x6, starting transfers between devices, hop(): return lax.ppermute(x, ('rows', 'cols'), pairs)  8.35 us
    ppermute x6, waiting for transfers between devices, hop(): return lax.ppermute(x, ('rows', 'cols'), pairs)  5.93 us
    ppermute x4, starting transfers between devices, swap(): return lax.ppermute(x, axis, [(i, i ^ bit) for i in range(size)])  3.92 us
  transfers between devices with their start and end apart: 10, of which 3 were waited for; matrix products, arithmetic and copies ran while one was open for 0% of the time, Pallas kernels for 4%

profile of v4, /device:TPU:1, one launch (start us, length us, event | category | flops | bytes accessed | tf_op | source)
XLA Modules:
  0.0 84.1 jit_solution(16905653589677638610)
XLA Ops:
  0.0 0.8 shard_map.46
  0.8 3.1 %collective-permute-start = (bf16[1,272,128]{2,1,0:T(8,128)(2,1)S(1)}, bf16[1,272,128]{2,1,0:T(8,128)(2,1)S(1)}, u32[]{:S(2)}, u32[]{:S(2)}) collective-permute-start(bf16[1,272,128]{2,1,0:T(8,128)(2,1)S(1)} %get-tuple-element.11.refs_0_), channel_id=1, source_target_pairs={{0,8},{1,9},{2,10},{3,11},{4,12},{5,13},{6,14},{7,15},{8,0},{9,1},... | collective-permute-start | bytes 208904 | tf_op jit(solution)/shard_map/ppermute | solution.py:229
  3.9 1.3 %collective-permute-start.1 = (bf16[1,272,128]{2,1,0:T(8,128)(2,1)S(1)}, bf16[1,272,128]{2,1,0:T(8,128)(2,1)S(1)}, u32[]{:S(2)}, u32[]{:S(2)}) collective-permute-start(bf16[1,272,128]{2,1,0:T(8,128)(2,1)S(1)} %get-tuple-element.11.refs_0_), channel_id=1, source_target_pairs={{0,4},{1,5},{2,6},{3,7},{4,0},{5,1},{6,2},{7,3},{8,12},{9,13},{10,... | collective-permute-start | bytes 208904 | tf_op jit(solution)/shard_map/ppermute | solution.py:229
  5.2 1.2 %collective-permute-start.2 = (bf16[1,272,128]{2,1,0:T(8,128)(2,1)S(1)}, bf16[1,272,128]{2,1,0:T(8,128)(2,1)S(1)}, u32[]{:S(2)}, u32[]{:S(2)}) collective-permute-start(bf16[1,272,128]{2,1,0:T(8,128)(2,1)S(1)} %get-tuple-element.11.refs_0_), channel_id=1, source_target_pairs={{0,2},{1,3},{2,0},{3,1},{4,6},{5,7},{6,4},{7,5},{8,10},{9,11},{10,... | collective-permute-start | bytes 208904 | tf_op jit(solution)/shard_map/ppermute | solution.py:229
  6.4 0.0 collective-permute-done.refs_1_.refs_0_
  6.4 1.2 %collective-permute-done.1.refs_2_.refs_1_ = bf16[1,272,128]{2,1,0:T(8,128)(2,1)S(1)} collective-permute-done((bf16[1,272,128]{2,1,0:T(8,128)(2,1)S(1)}, bf16[1,272,128]{2,1,0:T(8,128)(2,1)S(1)}, u32[]{:S(2)}, u32[]{:S(2)}) %collective-permute-start.1) | collective-permute-done | bytes 69664 | tf_op jit(solution)/shard_map/ppermute | solution.py:229
  7.6 1.0 %collective-permute-done.2.refs_3_ = bf16[1,272,128]{2,1,0:T(8,128)(2,1)S(1)} collective-permute-done((bf16[1,272,128]{2,1,0:T(8,128)(2,1)S(1)}, bf16[1,272,128]{2,1,0:T(8,128)(2,1)S(1)}, u32[]{:S(2)}, u32[]{:S(2)}) %collective-permute-start.2) | collective-permute-done | bytes 69664 | tf_op jit(solution)/shard_map/ppermute | solution.py:229
  8.7 0.0 copy-start
  8.7 2.2 %collective-permute-start.3 = (bf16[4,272,128]{2,1,0:T(8,128)(2,1)S(1)}, bf16[4,272,128]{2,1,0:T(8,128)(2,1)S(1)}, u32[]{:S(2)}, u32[]{:S(2)}) collective-permute-start(bf16[4,272,128]{2,1,0:T(8,128)(2,1)S(1)} %shard_map.47.refs_0_.refs_1_), channel_id=1, source_target_pairs={{0,1},{1,0},{2,3},{3,2},{4,5},{5,4},{6,7},{7,6},{8,9},{9,8},{10,11... | collective-permute-start | bytes 835592 | tf_op jit(solution)/shard_map/ppermute | solution.py:233
  10.9 1.3 %collective-permute-start.4 = (bf16[2,272,128]{2,1,0:T(8,128)(2,1)S(1)}, bf16[2,272,128]{2,1,0:T(8,128)(2,1)S(1)}, u32[]{:S(2)}, u32[]{:S(2)}) collective-permute-start(bf16[2,272,128]{2,1,0:T(8,128)(2,1)S(1)} %shard_map.50), channel_id=1, source_target_pairs={{0,2},{1,3},{2,0},{3,1},{4,6},{5,7},{6,4},{7,5},{8,10},{9,11},{10,... | collective-permute-start | bytes 417800 | tf_op jit(solution)/shard_map/ppermute | solution.py:229
  12.1 0.1 collective-permute-start.5
  12.3 1.3 %collective-permute-start.7 = (bf16[1,272,128]{2,1,0:T(8,128)(2,1)S(1)}, bf16[1,272,128]{2,1,0:T(8,128)(2,1)S(1)}, u32[]{:S(2)}, u32[]{:S(2)}) collective-permute-start(bf16[1,272,128]{2,1,0:T(8,128)(2,1)S(1)} %collective-permute-done.refs_1_.refs_0_), channel_id=1, source_target_pairs={{0,4},{1,5},{2,6},{3,7},{4,0},{5,1},{6,2},{7,3},{8,12},{9,13},{10,... | collective-permute-start | bytes 208904 | tf_op jit(solution)/shard_map/ppermute | solution.py:229
  13.6 3.7 %collective-permute-done.4.refs_0_.refs_5_ = bf16[2,272,128]{2,1,0:T(8,128)(2,1)S(1)} collective-permute-done((bf16[2,272,128]{2,1,0:T(8,128)(2,1)S(1)}, bf16[2,272,128]{2,1,0:T(8,128)(2,1)S(1)}, u32[]{:S(2)}, u32[]{:S(2)}) %collective-permute-start.4) | collective-permute-done | bytes 139296 | tf_op jit(solution)/shard_map/ppermute | solution.py:229
  17.3 1.3 %collective-permute-start.9 = (bf16[2,272,128]{2,1,0:T(8,128)(2,1)S(1)}, bf16[2,272,128]{2,1,0:T(8,128)(2,1)S(1)}, u32[]{:S(2)}, u32[]{:S(2)}) collective-permute-start(bf16[2,272,128]{2,1,0:T(8,128)(2,1)S(1)} %collective-permute-done.4.refs_0_.refs_5_), channel_id=1, source_target_pairs={{0,1},{1,0},{2,3},{3,2},{4,5},{5,4},{6,7},{7,6},{8,9},{9,8},{10,11... | collective-permute-start | bytes 417800 | tf_op jit(solution)/shard_map/ppermute | solution.py:233
  18.5 0.0 collective-permute-done.5.refs_1_.refs_3_
  18.5 0.0 collective-permute-start.6
  18.5 0.0 collective-permute-done.7.refs_0_.refs_6_
  18.5 0.5 collective-permute-start.8
  19.0 0.0 copy-done
  19.0 1.0 %shard_map.48 = (f32[1024,256]{1,0:T(8,128)S(1)}, f32[128,128]{1,0:T(8,128)S(1)}, bf16[1024,128]{1,0:T(8,128)(2,1)S(1)}) custom-call(bf16[128,1024]{1,0:T(8,128)(2,1)S(1)} %copy-done, f32[1,128]{1,0:T(1,128)S(1)} %get-tuple-element.10.pos_ref, bf16[4,272,128]{2,1,0:T(8,128)(2,1)S(1)} %shard_map.47.refs_0_.refs_1_), custom_call_target="tpu_custom_call" | custom-call | flops 268435456 | bytes 541184 | tf_op jit(solution)/shard_map/pallas_call | solution.py:29
  20.0 0.0 collective-permute-done.3.refs_0_.refs_2_
  20.0 0.8 shard_map.49.before_ref
  20.8 0.0 collective-permute-done.6.refs_2_.refs_4_
  20.8 0.8 shard_map.51.before_ref
  21.7 0.0 collective-permute-done.8.refs_1_.refs_7_
  21.7 0.5 shard_map.52.before_ref
  22.2 0.0 collective-permute-done.9.refs_0_
  22.3 61.8 %shard_map.53 = bf16[128,1024]{1,0:T(8,128)(2,1)} custom-call(bf16[1024,128]{1,0:T(8,128)(2,1)S(1)} %get-tuple-element.12.qs_ref, f32[128,128]{1,0:T(8,128)S(1)} %get-tuple-element.13.qpos_ref, f32[1024,256]{1,0:T(8,128)S(1)} %shard_map.52.before_ref, bf16[2,272,128]{2,1,0:T(8,128)(2,1)S(1)} %collective-permute-done.9.refs_0_, ...), custom_call_target="tpu_custom_call" | custom-call | flops 134217728 | bytes 2490368 | tf_op jit(solution)/shard_map/pallas_call | solution.py:29
  (2 shorter events, 0.0 us)
Async XLA Ops:
  0.8 5.6 %collective-permute-start = (bf16[1,272,128]{2,1,0:T(8,128)(2,1)S(1)}, bf16[1,272,128]{2,1,0:T(8,128)(2,1)S(1)}, u32[]{:S(2)}, u32[]{:S(2)}) collective-permute-start(bf16[1,272,128]{2,1,0:T(8,128)(2,1)S(1)} %get-tuple-element.11.refs_0_), channel_id=1, source_target_pairs={{0,8},{1,9},{2,10},{3,11},{4,12},{5,13},{6,14},{7,15},{8,0},{9,1},... | collective-permute-start | bytes 208904 | tf_op jit(solution)/shard_map/ppermute | solution.py:229
  3.9 3.7 %collective-permute-start.1 = (bf16[1,272,128]{2,1,0:T(8,128)(2,1)S(1)}, bf16[1,272,128]{2,1,0:T(8,128)(2,1)S(1)}, u32[]{:S(2)}, u32[]{:S(2)}) collective-permute-start(bf16[1,272,128]{2,1,0:T(8,128)(2,1)S(1)} %get-tuple-element.11.refs_0_), channel_id=1, source_target_pairs={{0,4},{1,5},{2,6},{3,7},{4,0},{5,1},{6,2},{7,3},{8,12},{9,13},{10,... | collective-permute-start | bytes 208904 | tf_op jit(solution)/shard_map/ppermute | solution.py:229
  5.2 3.5 %collective-permute-start.2 = (bf16[1,272,128]{2,1,0:T(8,128)(2,1)S(1)}, bf16[1,272,128]{2,1,0:T(8,128)(2,1)S(1)}, u32[]{:S(2)}, u32[]{:S(2)}) collective-permute-start(bf16[1,272,128]{2,1,0:T(8,128)(2,1)S(1)} %get-tuple-element.11.refs_0_), channel_id=1, source_target_pairs={{0,2},{1,3},{2,0},{3,1},{4,6},{5,7},{6,4},{7,5},{8,10},{9,11},{10,... | collective-permute-start | bytes 208904 | tf_op jit(solution)/shard_map/ppermute | solution.py:229
  8.7 10.3 %copy-start = (bf16[128,1024]{1,0:T(8,128)(2,1)S(1)}, bf16[128,1024]{1,0:T(8,128)(2,1)}, u32[]{:S(2)}) copy-start(bf16[128,1024]{1,0:T(8,128)(2,1)} %q_ref.1) | copy-start | bytes 786436
  8.7 11.3 %collective-permute-start.3 = (bf16[4,272,128]{2,1,0:T(8,128)(2,1)S(1)}, bf16[4,272,128]{2,1,0:T(8,128)(2,1)S(1)}, u32[]{:S(2)}, u32[]{:S(2)}) collective-permute-start(bf16[4,272,128]{2,1,0:T(8,128)(2,1)S(1)} %shard_map.47.refs_0_.refs_1_), channel_id=1, source_target_pairs={{0,1},{1,0},{2,3},{3,2},{4,5},{5,4},{6,7},{7,6},{8,9},{9,8},{10,11... | collective-permute-start | bytes 835592 | tf_op jit(solution)/shard_map/ppermute | solution.py:233
  10.9 6.4 %collective-permute-start.4 = (bf16[2,272,128]{2,1,0:T(8,128)(2,1)S(1)}, bf16[2,272,128]{2,1,0:T(8,128)(2,1)S(1)}, u32[]{:S(2)}, u32[]{:S(2)}) collective-permute-start(bf16[2,272,128]{2,1,0:T(8,128)(2,1)S(1)} %shard_map.50), channel_id=1, source_target_pairs={{0,2},{1,3},{2,0},{3,1},{4,6},{5,7},{6,4},{7,5},{8,10},{9,11},{10,... | collective-permute-start | bytes 417800 | tf_op jit(solution)/shard_map/ppermute | solution.py:229
  12.1 6.4 %collective-permute-start.5 = (bf16[1,272,128]{2,1,0:T(8,128)(2,1)S(1)}, bf16[1,272,128]{2,1,0:T(8,128)(2,1)S(1)}, u32[]{:S(2)}, u32[]{:S(2)}) collective-permute-start(bf16[1,272,128]{2,1,0:T(8,128)(2,1)S(1)} %collective-permute-done.refs_1_.refs_0_), channel_id=1, source_target_pairs={{0,6},{1,7},{2,4},{3,5},{4,2},{5,3},{6,0},{7,1},{8,14},{9,15},{10,... | collective-permute-start | bytes 208904 | tf_op jit(solution)/shard_map/ppermute | solution.py:229
  12.3 6.2 %collective-permute-start.7 = (bf16[1,272,128]{2,1,0:T(8,128)(2,1)S(1)}, bf16[1,272,128]{2,1,0:T(8,128)(2,1)S(1)}, u32[]{:S(2)}, u32[]{:S(2)}) collective-permute-start(bf16[1,272,128]{2,1,0:T(8,128)(2,1)S(1)} %collective-permute-done.refs_1_.refs_0_), channel_id=1, source_target_pairs={{0,4},{1,5},{2,6},{3,7},{4,0},{5,1},{6,2},{7,3},{8,12},{9,13},{10,... | collective-permute-start | bytes 208904 | tf_op jit(solution)/shard_map/ppermute | solution.py:229
  17.3 5.0 %collective-permute-start.9 = (bf16[2,272,128]{2,1,0:T(8,128)(2,1)S(1)}, bf16[2,272,128]{2,1,0:T(8,128)(2,1)S(1)}, u32[]{:S(2)}, u32[]{:S(2)}) collective-permute-start(bf16[2,272,128]{2,1,0:T(8,128)(2,1)S(1)} %collective-permute-done.4.refs_0_.refs_5_), channel_id=1, source_target_pairs={{0,1},{1,0},{2,3},{3,2},{4,5},{5,4},{6,7},{7,6},{8,9},{9,8},{10,11... | collective-permute-start | bytes 417800 | tf_op jit(solution)/shard_map/ppermute | solution.py:233
  18.5 2.3 %collective-permute-start.6 = (bf16[1,272,128]{2,1,0:T(8,128)(2,1)S(1)}, bf16[1,272,128]{2,1,0:T(8,128)(2,1)S(1)}, u32[]{:S(2)}, u32[]{:S(2)}) collective-permute-start(bf16[1,272,128]{2,1,0:T(8,128)(2,1)S(1)} %collective-permute-done.5.refs_1_.refs_3_), channel_id=1, source_target_pairs={{0,1},{1,0},{2,3},{3,2},{4,5},{5,4},{6,7},{7,6},{8,9},{9,8},{10,11... | collective-permute-start | bytes 208904 | tf_op jit(solution)/shard_map/ppermute | solution.py:233
  18.5 3.2 %collective-permute-start.8 = (bf16[1,272,128]{2,1,0:T(8,128)(2,1)S(1)}, bf16[1,272,128]{2,1,0:T(8,128)(2,1)S(1)}, u32[]{:S(2)}, u32[]{:S(2)}) collective-permute-start(bf16[1,272,128]{2,1,0:T(8,128)(2,1)S(1)} %collective-permute-done.7.refs_0_.refs_6_), channel_id=1, source_target_pairs={{0,1},{1,0},{2,3},{3,2},{4,5},{5,4},{6,7},{7,6},{8,9},{9,8},{10,11... | collective-permute-start | bytes 208904 | tf_op jit(solution)/shard_map/ppermute | solution.py:233

commit v5 on v4

--- a/solution.py
+++ b/solution.py
@@ -86,7 +86,7 @@
     )
 
 
-def absorb(qs_ref, query_pos, total, blocks, at, stack):
+def absorb(qs_ref, query_pos, total, blocks, at, stack, by_lane=False):
     pre = HEAD_DIM ** (-0.5) * math.log2(math.e)
     q = qs_ref[at, :]
     for j in range(0, len(blocks), 2):
@@ -95,16 +95,21 @@
         mask = jnp.concatenate([visible_of(*b, query_pos) for b in group], axis=1)
         mask = jnp.concatenate([mask] * stack, axis=0)
         weights = jnp.where(mask, jnp.exp2(scores * pre), 0.0).astype(jnp.bfloat16)
-        part = jnp.dot(
-            weights,
-            jnp.concatenate([values_of(*b) for b in group], axis=0),
-            preferred_element_type=jnp.float32,
-        )
+        values = jnp.concatenate([values_of(*b) for b in group], axis=0)
+        if by_lane:
+            part = jnp.dot(weights, values[:, :HEAD_DIM], preferred_element_type=jnp.float32)
+            wide = weights.astype(jnp.float32)
+            sums = wide[:, :LANES]
+            for j in range(LANES, wide.shape[1], LANES):
+                sums = sums + wide[:, j : j + LANES]
+            part = jnp.concatenate([part, sums], axis=1)
+        else:
+            part = jnp.dot(weights, values, preferred_element_type=jnp.float32)
         total = part if total is None else total + part
     return total
 
 
-def accumulate(qs_ref, query_pos, before, after, pieces, groups=None):
+def accumulate(qs_ref, query_pos, before, after, pieces, groups=None, by_lane=False):
     stack = 4 if HEADS % 4 == 0 else 1
     tokens = query_pos.shape[0]
     span = stack * tokens
@@ -114,14 +119,14 @@
         start = None if before is None else before[at, :]
         if small:
             blocks = [(p, i) for p in pieces for i in range(p.shape[0])]
-            after[at, :] = absorb(qs_ref, query_pos, start, blocks, at, stack)
+            after[at, :] = absorb(qs_ref, query_pos, start, blocks, at, stack, by_lane)
             continue
         after[at, :] = jnp.zeros((span, 2 * HEAD_DIM), jnp.float32) if start is None else start
         for p in pieces:
 
             def pair(i, carry, p=p):
                 blocks = [(p, 2 * i), (p, 2 * i + 1)]
-                after[at, :] = absorb(qs_ref, query_pos, after[at, :], blocks, at, stack)
+                after[at, :] = absorb(qs_ref, query_pos, after[at, :], blocks, at, stack, by_lane)
                 return carry
 
             lax.fori_loop(0, p.shape[0] // 2, pair, 0)
@@ -147,11 +152,15 @@
     qpos_ref[...] = jnp.transpose(
         jnp.broadcast_to(pos_ref[...], (LANES, tokens))
     )
-    accumulate(qs_ref, qpos_ref[...], None, acc_ref, refs[:count])
-
-
-def next_kernel(count, qs_ref, qpos_ref, before_ref, *refs):
-    accumulate(qs_ref, qpos_ref[...], before_ref, refs[count], refs[:count])
+    accumulate(qs_ref, qpos_ref[...], None, acc_ref, refs[:count], by_lane=True)
+
+
+def next_kernel(count, spread, qs_ref, qpos_ref, before_ref, *refs):
+    acc_ref = refs[count]
+    accumulate(qs_ref, qpos_ref[...], before_ref, acc_ref, refs[:count], by_lane=True)
+    if spread:
+        sums = jnp.sum(acc_ref[:, HEAD_DIM:], axis=1, keepdims=True)
+        acc_ref[:, HEAD_DIM:] = jnp.broadcast_to(sums, (sums.shape[0], HEAD_DIM))
 
 
 def last_kernel(count, qs_ref, qpos_ref, before_ref, *refs):
@@ -262,9 +271,9 @@
     def work(pieces):
         return 4 * HEADS * tokens * HEAD_DIM * tokens * sum(p.shape[0] for p in pieces)
 
-    def further(before, pieces):
+    def further(before, pieces, spread=False):
         return call(
-            functools.partial(next_kernel, len(pieces)), acc,
+            functools.partial(next_kernel, len(pieces), spread), acc,
             [qs, query_pos, before, *pieces], flops=work(pieces),
         )
 
@@ -289,7 +298,7 @@
     cz3 = swap(z3, "cols", cols, 1)
     czb = swap(zb, "cols", cols, 1)
     acc3 = further(acc2, [zb, xz3, cc])
-    acc4 = further(acc3, [z3, cz3])
+    acc4 = further(acc3, [z3, cz3], True)
     pieces = [czb, b1, cb1, xz3, cc, zb, z3, cz3]
     return call(
         functools.partial(last_kernel, 1),

time: 84.2 us -> 84.1 us (level)
  no operation moved by 1% of the time
where the time goes in v5:
time: 84.1 us; the launch traced here: 83.9 us
  Pallas kernels  65.7 us (78%)
  starting transfers between devices  12.3 us (15%)
  waiting for transfers between devices  5.94 us (7%)
    pallas_call x8, Pallas kernels, call(): pl.pallas_call(kernel, out_shape=out_shape, in_specs=[VMEM] * len(operand...  65.7 us
    ppermute x6, starting transfers between devices, hop(): return lax.ppermute(x, ('rows', 'cols'), pairs)  8.35 us
    ppermute x6, waiting for transfers between devices, hop(): return lax.ppermute(x, ('rows', 'cols'), pairs)  5.93 us
    ppermute x4, starting transfers between devices, swap(): return lax.ppermute(x, axis, [(i, i ^ bit) for i in range(size)])  3.92 us
  transfers between devices with their start and end apart: 10, of which 3 were waited for; matrix products, arithmetic and copies ran while one was open for 0% of the time, Pallas kernels for 4%

profile of v5, /device:TPU:1, one launch (start us, length us, event | category | flops | bytes accessed | tf_op | source)
XLA Modules:
  0.0 83.9 jit_solution(7065769944872829862)
XLA Ops:
  0.0 0.8 shard_map.46
  0.8 3.1 %collective-permute-start = (bf16[1,272,128]{2,1,0:T(8,128)(2,1)S(1)}, bf16[1,272,128]{2,1,0:T(8,128)(2,1)S(1)}, u32[]{:S(2)}, u32[]{:S(2)}) collective-permute-start(bf16[1,272,128]{2,1,0:T(8,128)(2,1)S(1)} %get-tuple-element.11.refs_0_), channel_id=1, source_target_pairs={{0,8},{1,9},{2,10},{3,11},{4,12},{5,13},{6,14},{7,15},{8,0},{9,1},... | collective-permute-start | bytes 208904 | tf_op jit(solution)/shard_map/ppermute | solution.py:238
  3.9 1.3 %collective-permute-start.1 = (bf16[1,272,128]{2,1,0:T(8,128)(2,1)S(1)}, bf16[1,272,128]{2,1,0:T(8,128)(2,1)S(1)}, u32[]{:S(2)}, u32[]{:S(2)}) collective-permute-start(bf16[1,272,128]{2,1,0:T(8,128)(2,1)S(1)} %get-tuple-element.11.refs_0_), channel_id=1, source_target_pairs={{0,4},{1,5},{2,6},{3,7},{4,0},{5,1},{6,2},{7,3},{8,12},{9,13},{10,... | collective-permute-start | bytes 208904 | tf_op jit(solution)/shard_map/ppermute | solution.py:238
  5.2 1.2 %collective-permute-start.2 = (bf16[1,272,128]{2,1,0:T(8,128)(2,1)S(1)}, bf16[1,272,128]{2,1,0:T(8,128)(2,1)S(1)}, u32[]{:S(2)}, u32[]{:S(2)}) collective-permute-start(bf16[1,272,128]{2,1,0:T(8,128)(2,1)S(1)} %get-tuple-element.11.refs_0_), channel_id=1, source_target_pairs={{0,2},{1,3},{2,0},{3,1},{4,6},{5,7},{6,4},{7,5},{8,10},{9,11},{10,... | collective-permute-start | bytes 208904 | tf_op jit(solution)/shard_map/ppermute | solution.py:238
  6.4 0.0 collective-permute-done.refs_1_.refs_0_
  6.4 1.2 %collective-permute-done.1.refs_2_.refs_1_ = bf16[1,272,128]{2,1,0:T(8,128)(2,1)S(1)} collective-permute-done((bf16[1,272,128]{2,1,0:T(8,128)(2,1)S(1)}, bf16[1,272,128]{2,1,0:T(8,128)(2,1)S(1)}, u32[]{:S(2)}, u32[]{:S(2)}) %collective-permute-start.1) | collective-permute-done | bytes 69664 | tf_op jit(solution)/shard_map/ppermute | solution.py:238
  7.6 1.0 %collective-permute-done.2.refs_3_ = bf16[1,272,128]{2,1,0:T(8,128)(2,1)S(1)} collective-permute-done((bf16[1,272,128]{2,1,0:T(8,128)(2,1)S(1)}, bf16[1,272,128]{2,1,0:T(8,128)(2,1)S(1)}, u32[]{:S(2)}, u32[]{:S(2)}) %collective-permute-start.2) | collective-permute-done | bytes 69664 | tf_op jit(solution)/shard_map/ppermute | solution.py:238
  8.7 0.0 copy-start
  8.7 2.2 %collective-permute-start.3 = (bf16[4,272,128]{2,1,0:T(8,128)(2,1)S(1)}, bf16[4,272,128]{2,1,0:T(8,128)(2,1)S(1)}, u32[]{:S(2)}, u32[]{:S(2)}) collective-permute-start(bf16[4,272,128]{2,1,0:T(8,128)(2,1)S(1)} %shard_map.47.refs_0_.refs_1_), channel_id=1, source_target_pairs={{0,1},{1,0},{2,3},{3,2},{4,5},{5,4},{6,7},{7,6},{8,9},{9,8},{10,11... | collective-permute-start | bytes 835592 | tf_op jit(solution)/shard_map/ppermute | solution.py:242
  10.9 1.3 %collective-permute-start.4 = (bf16[2,272,128]{2,1,0:T(8,128)(2,1)S(1)}, bf16[2,272,128]{2,1,0:T(8,128)(2,1)S(1)}, u32[]{:S(2)}, u32[]{:S(2)}) collective-permute-start(bf16[2,272,128]{2,1,0:T(8,128)(2,1)S(1)} %shard_map.50), channel_id=1, source_target_pairs={{0,2},{1,3},{2,0},{3,1},{4,6},{5,7},{6,4},{7,5},{8,10},{9,11},{10,... | collective-permute-start | bytes 417800 | tf_op jit(solution)/shard_map/ppermute | solution.py:238
  12.1 0.1 collective-permute-start.5
  12.3 1.3 %collective-permute-start.7 = (bf16[1,272,128]{2,1,0:T(8,128)(2,1)S(1)}, bf16[1,272,128]{2,1,0:T(8,128)(2,1)S(1)}, u32[]{:S(2)}, u32[]{:S(2)}) collective-permute-start(bf16[1,272,128]{2,1,0:T(8,128)(2,1)S(1)} %collective-permute-done.refs_1_.refs_0_), channel_id=1, source_target_pairs={{0,4},{1,5},{2,6},{3,7},{4,0},{5,1},{6,2},{7,3},{8,12},{9,13},{10,... | collective-permute-start | bytes 208904 | tf_op jit(solution)/shard_map/ppermute | solution.py:238
  13.6 3.7 %collective-permute-done.4.refs_0_.refs_5_ = bf16[2,272,128]{2,1,0:T(8,128)(2,1)S(1)} collective-permute-done((bf16[2,272,128]{2,1,0:T(8,128)(2,1)S(1)}, bf16[2,272,128]{2,1,0:T(8,128)(2,1)S(1)}, u32[]{:S(2)}, u32[]{:S(2)}) %collective-permute-start.4) | collective-permute-done | bytes 139296 | tf_op jit(solution)/shard_map/ppermute | solution.py:238
  17.3 1.3 %collective-permute-start.9 = (bf16[2,272,128]{2,1,0:T(8,128)(2,1)S(1)}, bf16[2,272,128]{2,1,0:T(8,128)(2,1)S(1)}, u32[]{:S(2)}, u32[]{:S(2)}) collective-permute-start(bf16[2,272,128]{2,1,0:T(8,128)(2,1)S(1)} %collective-permute-done.4.refs_0_.refs_5_), channel_id=1, source_target_pairs={{0,1},{1,0},{2,3},{3,2},{4,5},{5,4},{6,7},{7,6},{8,9},{9,8},{10,11... | collective-permute-start | bytes 417800 | tf_op jit(solution)/shard_map/ppermute | solution.py:242
  18.5 0.0 collective-permute-done.5.refs_1_.refs_3_
  18.5 0.0 collective-permute-start.6
  18.5 0.0 collective-permute-done.7.refs_0_.refs_6_
  18.5 0.5 collective-permute-start.8
  19.0 0.0 copy-done
  19.0 0.8 shard_map.48
  19.9 0.0 collective-permute-done.3.refs_0_.refs_2_
  19.9 0.8 shard_map.49.before_ref
  20.7 0.0 collective-permute-done.6.refs_2_.refs_4_
  20.7 0.8 %shard_map.51.before_ref = f32[1024,256]{1,0:T(8,128)S(1)} custom-call(bf16[1024,128]{1,0:T(8,128)(2,1)S(1)} %get-tuple-element.12.qs_ref, f32[128,128]{1,0:T(8,128)S(1)} %get-tuple-element.13.qpos_ref, f32[1024,256]{1,0:T(8,128)S(1)} %shard_map.49.before_ref, bf16[2,272,128]{2,1,0:T(8,128)(2,1)S(1)} %collective-permute-done.4.refs_0_.refs_5_, ...), custom_call_target="tpu_custom_call" | custom-call | flops 268435456 | bytes 1654784 | tf_op jit(solution)/shard_map/pallas_call | solution.py:29
  21.6 0.0 collective-permute-done.8.refs_1_.refs_7_
  21.6 0.6 shard_map.52.before_ref
  22.1 0.0 collective-permute-done.9.refs_0_
  22.1 61.8 %shard_map.53 = bf16[128,1024]{1,0:T(8,128)(2,1)} custom-call(bf16[1024,128]{1,0:T(8,128)(2,1)S(1)} %get-tuple-element.12.qs_ref, f32[128,128]{1,0:T(8,128)S(1)} %get-tuple-element.13.qpos_ref, f32[1024,256]{1,0:T(8,128)S(1)} %shard_map.52.before_ref, bf16[2,272,128]{2,1,0:T(8,128)(2,1)S(1)} %collective-permute-done.9.refs_0_, ...), custom_call_target="tpu_custom_call" | custom-call | flops 134217728 | bytes 2490368 | tf_op jit(solution)/shard_map/pallas_call | solution.py:29
  (2 shorter events, 0.0 us)
Async XLA Ops:
  0.8 5.6 %collective-permute-start = (bf16[1,272,128]{2,1,0:T(8,128)(2,1)S(1)}, bf16[1,272,128]{2,1,0:T(8,128)(2,1)S(1)}, u32[]{:S(2)}, u32[]{:S(2)}) collective-permute-start(bf16[1,272,128]{2,1,0:T(8,128)(2,1)S(1)} %get-tuple-element.11.refs_0_), channel_id=1, source_target_pairs={{0,8},{1,9},{2,10},{3,11},{4,12},{5,13},{6,14},{7,15},{8,0},{9,1},... | collective-permute-start | bytes 208904 | tf_op jit(solution)/shard_map/ppermute | solution.py:238
  3.9 3.7 %collective-permute-start.1 = (bf16[1,272,128]{2,1,0:T(8,128)(2,1)S(1)}, bf16[1,272,128]{2,1,0:T(8,128)(2,1)S(1)}, u32[]{:S(2)}, u32[]{:S(2)}) collective-permute-start(bf16[1,272,128]{2,1,0:T(8,128)(2,1)S(1)} %get-tuple-element.11.refs_0_), channel_id=1, source_target_pairs={{0,4},{1,5},{2,6},{3,7},{4,0},{5,1},{6,2},{7,3},{8,12},{9,13},{10,... | collective-permute-start | bytes 208904 | tf_op jit(solution)/shard_map/ppermute | solution.py:238
  5.2 3.5 %collective-permute-start.2 = (bf16[1,272,128]{2,1,0:T(8,128)(2,1)S(1)}, bf16[1,272,128]{2,1,0:T(8,128)(2,1)S(1)}, u32[]{:S(2)}, u32[]{:S(2)}) collective-permute-start(bf16[1,272,128]{2,1,0:T(8,128)(2,1)S(1)} %get-tuple-element.11.refs_0_), channel_id=1, source_target_pairs={{0,2},{1,3},{2,0},{3,1},{4,6},{5,7},{6,4},{7,5},{8,10},{9,11},{10,... | collective-permute-start | bytes 208904 | tf_op jit(solution)/shard_map/ppermute | solution.py:238
  8.7 10.3 %copy-start = (bf16[128,1024]{1,0:T(8,128)(2,1)S(1)}, bf16[128,1024]{1,0:T(8,128)(2,1)}, u32[]{:S(2)}) copy-start(bf16[128,1024]{1,0:T(8,128)(2,1)} %q_ref.1) | copy-start | bytes 786436
  8.7 11.2 %collective-permute-start.3 = (bf16[4,272,128]{2,1,0:T(8,128)(2,1)S(1)}, bf16[4,272,128]{2,1,0:T(8,128)(2,1)S(1)}, u32[]{:S(2)}, u32[]{:S(2)}) collective-permute-start(bf16[4,272,128]{2,1,0:T(8,128)(2,1)S(1)} %shard_map.47.refs_0_.refs_1_), channel_id=1, source_target_pairs={{0,1},{1,0},{2,3},{3,2},{4,5},{5,4},{6,7},{7,6},{8,9},{9,8},{10,11... | collective-permute-start | bytes 835592 | tf_op jit(solution)/shard_map/ppermute | solution.py:242
  10.9 6.4 %collective-permute-start.4 = (bf16[2,272,128]{2,1,0:T(8,128)(2,1)S(1)}, bf16[2,272,128]{2,1,0:T(8,128)(2,1)S(1)}, u32[]{:S(2)}, u32[]{:S(2)}) collective-permute-start(bf16[2,272,128]{2,1,0:T(8,128)(2,1)S(1)} %shard_map.50), channel_id=1, source_target_pairs={{0,2},{1,3},{2,0},{3,1},{4,6},{5,7},{6,4},{7,5},{8,10},{9,11},{10,... | collective-permute-start | bytes 417800 | tf_op jit(solution)/shard_map/ppermute | solution.py:238
  12.1 6.4 %collective-permute-start.5 = (bf16[1,272,128]{2,1,0:T(8,128)(2,1)S(1)}, bf16[1,272,128]{2,1,0:T(8,128)(2,1)S(1)}, u32[]{:S(2)}, u32[]{:S(2)}) collective-permute-start(bf16[1,272,128]{2,1,0:T(8,128)(2,1)S(1)} %collective-permute-done.refs_1_.refs_0_), channel_id=1, source_target_pairs={{0,6},{1,7},{2,4},{3,5},{4,2},{5,3},{6,0},{7,1},{8,14},{9,15},{10,... | collective-permute-start | bytes 208904 | tf_op jit(solution)/shard_map/ppermute | solution.py:238
  12.3 6.2 %collective-permute-start.7 = (bf16[1,272,128]{2,1,0:T(8,128)(2,1)S(1)}, bf16[1,272,128]{2,1,0:T(8,128)(2,1)S(1)}, u32[]{:S(2)}, u32[]{:S(2)}) collective-permute-start(bf16[1,272,128]{2,1,0:T(8,128)(2,1)S(1)} %collective-permute-done.refs_1_.refs_0_), channel_id=1, source_target_pairs={{0,4},{1,5},{2,6},{3,7},{4,0},{5,1},{6,2},{7,3},{8,12},{9,13},{10,... | collective-permute-start | bytes 208904 | tf_op jit(solution)/shard_map/ppermute | solution.py:238
  17.3 4.9 %collective-permute-start.9 = (bf16[2,272,128]{2,1,0:T(8,128)(2,1)S(1)}, bf16[2,272,128]{2,1,0:T(8,128)(2,1)S(1)}, u32[]{:S(2)}, u32[]{:S(2)}) collective-permute-start(bf16[2,272,128]{2,1,0:T(8,128)(2,1)S(1)} %collective-permute-done.4.refs_0_.refs_5_), channel_id=1, source_target_pairs={{0,1},{1,0},{2,3},{3,2},{4,5},{5,4},{6,7},{7,6},{8,9},{9,8},{10,11... | collective-permute-start | bytes 417800 | tf_op jit(solution)/shard_map/ppermute | solution.py:242
  18.5 2.2 %collective-permute-start.6 = (bf16[1,272,128]{2,1,0:T(8,128)(2,1)S(1)}, bf16[1,272,128]{2,1,0:T(8,128)(2,1)S(1)}, u32[]{:S(2)}, u32[]{:S(2)}) collective-permute-start(bf16[1,272,128]{2,1,0:T(8,128)(2,1)S(1)} %collective-permute-done.5.refs_1_.refs_3_), channel_id=1, source_target_pairs={{0,1},{1,0},{2,3},{3,2},{4,5},{5,4},{6,7},{7,6},{8,9},{9,8},{10,11... | collective-permute-start | bytes 208904 | tf_op jit(solution)/shard_map/ppermute | solution.py:242
  18.5 3.0 %collective-permute-start.8 = (bf16[1,272,128]{2,1,0:T(8,128)(2,1)S(1)}, bf16[1,272,128]{2,1,0:T(8,128)(2,1)S(1)}, u32[]{:S(2)}, u32[]{:S(2)}) collective-permute-start(bf16[1,272,128]{2,1,0:T(8,128)(2,1)S(1)} %collective-permute-done.7.refs_0_.refs_6_), channel_id=1, source_target_pairs={{0,1},{1,0},{2,3},{3,2},{4,5},{5,4},{6,7},{7,6},{8,9},{9,8},{10,11... | collective-permute-start | bytes 208904 | tf_op jit(solution)/shard_map/ppermute | solution.py:242
